TPU v7x, 512 devices: a whole 4x8x8 slice. The times are simulated.
512 devices in a mesh: prow: 16 (over z_lo, x, core), pcol: 32 (over y, z_hi).
Axes of the slice: x: 4, y: 8, z: 8 (z_hi: 4, z_lo: 2; z = z_hi * 2 + z_lo), core: 2. Of those that a mesh axis runs over, the one named last changes fastest.
Arguments:
- matrix: float32 [6, 16, 128, 3, 32, 128], P(None, 'prow', None, None, 'pcol'), may hold values from -1 to 40, as said below
- row_codes: int32 [6, 16, 128], P(None, 'prow'), may hold values from 1 to 8
- col_codes: int32 [3, 32, 128], P(None, 'pcol'), may hold values from 1 to 8
- fault_tiles: int32 [96, 2], replicated, may hold values from 0 to 95, as said below
- fault_cells: int32 [96, 2], replicated, may hold values from 0 to 127
- fault_bits: int32 [96], replicated, may hold values from 1 to 2
Outputs:
- factored: float32 [6, 16, 128, 3, 32, 128], P(None, 'prow', None, None, 'pcol')
- col_check: float32 [3, 32, 128], P(None, 'pcol')
- row_check: float32 [6, 16, 128], P(None, 'prow')
- col_flags: float32 [3, 32], P(None, 'pcol')
- row_flags: float32 [6, 16], P(None, 'prow')
Inputs may be any that keep to these rules, and one draw needn't show every extreme that they name: `matrix`: symmetric positive definite. `fault_tiles`: each tile row index appears in exactly one fault, and so does each tile column index.
All inputs are finite; a program needn't handle non-finite values.
Results may differ from a plain program's by a relative error of at most 0.0003.
Values sent between devices are 32-bit elements; how exact they have to be, the bound alone decides.
No kernel may reach another device: no remote copies, remote signals or barrier semaphores. Data moves between devices by JAX's collectives and lax.ppermute only.
A program may use at most 64 MiB of HBM per device.

v0:
```python
import jax
import jax.numpy as jnp
from jax import lax
from jax.sharding import PartitionSpec as P

STEPS = 2


precise = lax.Precision.HIGHEST


def broadcast(block, axis, holder):
    block = jnp.where(lax.axis_index(axis) == holder, block, jnp.zeros_like(block))
    return lax.psum(block, axis)


def factor_diagonal(diagonal):
    factor = jnp.linalg.cholesky(diagonal)
    identity = jnp.eye(diagonal.shape[0], dtype=jnp.float32)
    inverse = jax.scipy.linalg.solve_triangular(factor, identity, lower=True)
    return (factor, inverse)


def form_panel(col_blocks, tile_ids, factor, inverse, step_index):
    product = jnp.einsum("iab,cb->iac", col_blocks, inverse, precision=precise)
    chosen = jnp.where((tile_ids == step_index)[:, None, None], factor[None], 0.0)
    return jnp.where((tile_ids > step_index)[:, None, None], product, chosen)


def update_range(blocks, trailing_rows, trailing_cols):
    update = jnp.einsum("iab,jcb->iajc", trailing_rows, trailing_cols, precision=precise)
    return blocks - update


def local(matrix, row_codes, col_codes, fault_tiles, fault_cells, fault_bits):
    grid_rows = lax.axis_size("prow")
    grid_cols = lax.axis_size("pcol")
    grid_row = lax.axis_index("prow")
    grid_col = lax.axis_index("pcol")
    tile_rows, _, tile_size, tile_cols, _, _ = matrix.shape
    blocks = matrix.reshape(tile_rows, tile_size, tile_cols, tile_size)
    row_weights = row_codes.reshape(tile_rows, tile_size).astype(jnp.float32) * 0.25
    col_weights = col_codes.reshape(tile_cols, tile_size).astype(jnp.float32) * 0.25
    tile_row = jnp.arange(tile_rows, dtype=jnp.int32) * grid_rows + grid_row
    tile_col = jnp.arange(tile_cols, dtype=jnp.int32) * grid_cols + grid_col
    col_check = lax.psum(jnp.einsum("ia,iajc->jc", row_weights, blocks, precision=precise), "prow")
    row_check = lax.psum(jnp.einsum("iajc,jc->ia", blocks, col_weights, precision=precise), "pcol")
    magnitude = jnp.exp2(fault_bits.astype(jnp.float32) - 1.0)
    fault_rows = fault_tiles[:, 0] * tile_size + fault_cells[:, 0]
    fault_cols = fault_tiles[:, 1] * tile_size + fault_cells[:, 1]
    offsets = jnp.arange(tile_size, dtype=jnp.int32)
    local_rows = (tile_row[:, None] * tile_size + offsets[None, :]).reshape(-1)
    local_cols = (tile_col[:, None] * tile_size + offsets[None, :]).reshape(-1)
    hit_rows = (fault_rows[:, None] == local_rows[None, :]).astype(jnp.float32) * magnitude[:, None]
    hit_cols = (fault_cols[:, None] == local_cols[None, :]).astype(jnp.float32)
    faults_added = jnp.dot(hit_rows.T, hit_cols, precision=precise)
    blocks = blocks + faults_added.reshape(tile_rows, tile_size, tile_cols, tile_size)
    picked = (
        jnp.arange(tile_cols, dtype=jnp.int32) * (grid_cols // grid_rows) + grid_col // grid_rows
    )
    owner_row = grid_col % grid_rows

    def factor_panel(blocks, row_check, col_check, step_index):
        root_row = step_index % grid_rows
        root_col = step_index % grid_cols
        local_row = step_index // grid_rows
        local_col = step_index // grid_cols
        diagonal = broadcast(blocks[local_row, :, local_col, :], "prow", root_row)
        factor, inverse = factor_diagonal(diagonal)
        own_rows = form_panel(blocks[:, :, local_col, :], tile_row, factor, inverse, step_index)
        own_check = jnp.dot(inverse, col_check[local_col], precision=precise)
        panel_rows, new_check = (
            broadcast(own_rows, "pcol", root_col),
            broadcast(own_check, "pcol", root_col),
        )
        across = broadcast(jnp.take(panel_rows, picked, axis=0), "prow", owner_row)
        owner_col = grid_col == root_col
        shift_term = jnp.einsum("jab,ja->b", across, col_weights, precision=precise)
        shift_term = shift_term - jnp.where(owner_col, col_weights[local_col], 0.0)
        shift_vector = lax.psum(shift_term, "pcol")
        row_check = row_check - jnp.einsum("iab,b->ia", panel_rows, shift_vector, precision=precise)
        col_update = jnp.einsum("jab,b->ja", across, new_check, precision=precise)
        col_check = col_check - jnp.where((tile_col > step_index)[:, None], col_update, 0.0)
        col_check = col_check.at[local_col].set(
            jnp.where(owner_col, new_check, col_check[local_col])
        )
        trailing_rows = jnp.where((tile_row > step_index)[:, None, None], panel_rows, 0.0)
        trailing_cols = jnp.where((tile_col > step_index)[:, None, None], across, 0.0)
        return (panel_rows, trailing_rows, trailing_cols, row_check, col_check)

    current = factor_panel(blocks, row_check, col_check, 0)
    for step_index in range(STEPS):
        panel_rows, trailing_rows, trailing_cols, row_check, col_check = current
        blocks = update_range(blocks, trailing_rows, trailing_cols)
        if step_index + 1 < STEPS:
            current = factor_panel(blocks, row_check, col_check, step_index + 1)
        settle_blocks = blocks
        settle_local_col = step_index // grid_cols
        previous = settle_blocks[:, :, settle_local_col, :]
        settle_blocks = settle_blocks.at[:, :, settle_local_col, :].set(
            jnp.where(grid_col == step_index % grid_cols, panel_rows, previous)
        )
        cleared = (tile_row == step_index)[:, None, None, None] & (tile_col > step_index)[
            None, None, :, None
        ]
        blocks = jnp.where(cleared, 0.0, settle_blocks)
    col_found = lax.psum(jnp.einsum("ia,iajc->jc", row_weights, blocks, precision=precise), "prow")
    row_found = lax.psum(jnp.einsum("iajc,jc->ia", blocks, col_weights, precision=precise), "pcol")
    col_flags = jnp.max(jnp.abs(col_check - col_found), axis=1)
    row_flags = jnp.max(jnp.abs(row_check - row_found), axis=1)
    return (
        blocks.reshape(matrix.shape),
        col_check.reshape(tile_cols, 1, tile_size),
        row_check.reshape(tile_rows, 1, tile_size),
        col_flags.reshape(tile_cols, 1),
        row_flags.reshape(tile_rows, 1),
    )


def solution(mesh):
    return jax.shard_map(
        local,
        mesh=mesh,
        in_specs=(
            P(None, "prow", None, None, "pcol", None),
            P(None, "prow", None),
            P(None, "pcol", None),
            P(),
            P(),
            P(),
        ),
        out_specs=(
            P(None, "prow", None, None, "pcol", None),
            P(None, "pcol", None),
            P(None, "prow", None),
            P(None, "pcol"),
            P(None, "prow"),
        ),
        check_vma=False,
    )
```

profile of v0, /device:TPU:64, one launch (start us, length us, event | category | flops | bytes accessed | tf_op | source)
XLA Modules:
  0.0 1383.4 jit_solution(15013393687045354452)
XLA Ops:
  7.2 0.7 multiply_exponential_fusion
  8.1 0.8 add_bitcast_fusion.2
  8.8 0.7 fusion.15
  9.6 1.3 reshape.353
  10.9 0.3 copy-done.7
  11.2 0.9 copy.30
  12.1 1.7 bitcast_add_fusion
  13.8 0.6 fusion.42
  14.6 0.6 broadcast_compare_fusion.4
  15.2 0.6 broadcast_and_fusion
  15.9 118.3 %all-reduce.9.cloned.1.call-done = f32[128,128]{0,1:T(8,128)} async-done(((f32[128,128]{0,1:T(8,128)}), f32[128,128]{0,1:T(8,128)}) %all-reduce.9.cloned.1.call-update) | async-done | bytes 65552 | tf_op jit(solution)/shard_map/psum | solution.py:14
  134.2 0.9 copy.33
  135.1 0.9 fusion.48
  135.9 11.7 cholesky.44
  147.7 0.6 compare_reduce_fusion.1
  148.3 0.7 select_bitcast_fusion.1
  149.0 9.8 custom-call.6
  158.8 0.3 fusion.37
  159.2 1.2 fusion.1
  160.6 0.7 fusion.2
  161.3 309.4 %all-reduce.11.cloned.1.call-done = f32[6,128,128]{1,2,0:T(8,128)} async-done(((f32[6,128,128]{1,2,0:T(8,128)}), f32[6,128,128]{1,2,0:T(8,128)}) %all-reduce.11.cloned.1.call-update) | async-done | bytes 393232 | tf_op jit(solution)/shard_map/psum | solution.py:14
  470.7 1.6 gather_fusion
  472.2 0.8 select_select_fusion.1
  473.1 0.7 broadcast_and_fusion.1
  473.8 118.5 %all-reduce.13.cloned.1.call-done = f32[3,128,128]{1,2,0:T(8,128)} async-done(((f32[3,128,128]{1,2,0:T(8,128)}), f32[3,128,128]{1,2,0:T(8,128)}) %all-reduce.13.cloned.1.call-update) | async-done | bytes 196624 | tf_op jit(solution)/shard_map/psum | solution.py:14
  592.2 2.3 convolution_subtract_fusion.1
  594.6 0.6 fusion.41
  595.2 0.2 all-reduce.17.cloned.1.call-start
  595.5 1.7 convolution_reduce_fusion.1
  597.2 115.8 %all-reduce.15.cloned.1.call-done = f32[128,128]{0,1:T(8,128)} async-done(((f32[128,128]{0,1:T(8,128)}), f32[128,128]{0,1:T(8,128)}) %all-reduce.15.cloned.1.call-update) | async-done | bytes 65552 | tf_op jit(solution)/shard_map/psum | solution.py:14
  712.9 0.9 copy.42
  713.9 0.9 fusion.45
  714.7 11.7 cholesky.55
  726.5 0.6 compare_reduce_fusion
  727.1 0.7 select_bitcast_fusion
  727.8 9.8 custom-call.7
  737.6 0.3 fusion.35
  738.0 1.2 fusion
  739.4 0.8 fusion.7
  740.2 309.2 %all-reduce.17.cloned.1.call-done = f32[6,128,128]{1,2,0:T(8,128)} async-done(((f32[6,128,128]{1,2,0:T(8,128)}), f32[6,128,128]{1,2,0:T(8,128)}) %all-reduce.17.cloned.1.call-update) | async-done | bytes 393232 | tf_op jit(solution)/shard_map/psum | solution.py:14
  1049.4 1.7 gather_fusion.1
  1051.2 0.8 select_select_fusion
  1052.0 119.1 %all-reduce.19.cloned.1.call-done = f32[3,128,128]{1,2,0:T(8,128)} async-done(((f32[3,128,128]{1,2,0:T(8,128)}), f32[3,128,128]{1,2,0:T(8,128)}) %all-reduce.19.cloned.1.call-update) | async-done | bytes 196624 | tf_op jit(solution)/shard_map/psum | solution.py:14
  1171.1 2.2 convolution_subtract_fusion
  1173.4 0.6 copy-done.15
  1174.1 0.1 fusion.93
  1174.3 0.5 copy-done.14
  1174.8 1.1 convolution_reduce_fusion
  1176.0 30.0 %all-reduce.1 = (f32[3,128]{1,0:T(4,128)S(1)}, f32[3,128]{1,0:T(4,128)S(1)}) all-reduce(f32[3,128]{1,0:T(4,128)S(1)} %bitcast.205, f32[3,128]{1,0:T(4,128)S(1)} %bitcast.206), channel_id=1, replica_groups=mesh['prow'=16,'pcol'=32] {'prow'}, use_global_device_ids=true, to_apply=%region_8.12 | all-reduce | flops 768 | bytes 6144 | tf_op jit(solution)/shard_map/psum | solution.py:46
  1206.0 0.2 fusion.5
  1206.2 83.8 %psum.105 = f32[128]{0:T(128)S(1)} all-reduce(f32[128]{0:T(128)S(1)} %fusion.5), channel_id=1, replica_groups=mesh['prow'=16,'pcol'=32] {'pcol'}, use_global_device_ids=true, to_apply=%region_9.13 | all-reduce | flops 128 | bytes 1024 | tf_op jit(solution)/shard_map/psum | solution.py:14
  1290.0 0.2 fusion.71
  1290.3 0.2 fusion.4
  1290.5 0.8 fusion.56
  1291.3 2.6 copy.50
  1294.0 0.3 fusion.6
  1294.2 78.9 %all-reduce = (f32[128]{0:T(128)S(1)}, f32[6,128]{1,0:T(8,128)S(1)}, f32[128]{0:T(128)S(1)}, f32[128]{0:T(128)S(1)}, f32[6,128]{1,0:T(8,128)S(1)}) all-reduce(f32[128]{0:T(128)S(1)} %fusion.4, f32[6,128]{1,0:T(8,128)S(1)} %bitcast.203, f32[128]{0:T(128)S(1)} %fusion.6, ...), channel_id=1, replica_groups=mesh['prow'=16,'pcol'=32] {'pcol'}, use_global_device_ids=true, to_apply=%region_10.14 | all-reduce | flops 1920 | bytes 15360 | tf_op jit(solution)/shard_map/psum | solution.py:14
  1373.2 0.2 fusion.68
  1373.5 0.6 reshape.358
  1374.1 0.6 abs_reduce_fusion.1
  1374.7 0.3 fusion.66
  1375.0 0.3 fusion.64
  1375.3 0.7 abs_reduce_fusion
  1376.0 0.6 reshape.359
  (95 shorter events, 1.4 us)
Async XLA Ops:
  7.2 127.0 %all-reduce.9.cloned.1.call-start = ((), (), s32[]{:S(2)}) async-start(), calls=%async_computation | async-start | bytes 131072 | tf_op jit(solution)/shard_map/psum | solution.py:14
  9.6 1.7 copy-start.7
  12.1 3.1 copy-start.12
  14.5 456.2 %all-reduce.11.cloned.1.call-start = ((), (), s32[]{:S(2)}) async-start(), calls=%async_computation.1 | async-start | bytes 786432 | tf_op jit(solution)/shard_map/psum | solution.py:14
  14.6 1.3 copy-start.20
  14.6 458.5 %copy-start.18 = (pred[3]{0:T(512)(128)(4,1)}, pred[3]{0:T(512)(128)(4,1)S(1)}, u32[]{:S(2)}) copy-start(pred[3]{0:T(512)(128)(4,1)S(1)} %broadcast_compare_fusion.3) | copy-start | bytes 13
  14.6 146.6 %copy-start.29 = (pred[6]{0:T(512)(128)(4,1)}, pred[6]{0:T(512)(128)(4,1)S(1)}, u32[]{:S(2)}) copy-start(pred[6]{0:T(512)(128)(4,1)S(1)} %get-tuple-element.81) | copy-start | bytes 22
  15.2 457.9 %copy-start.27 = (pred[6]{0:T(512)(128)(4,1)}, pred[6]{0:T(512)(128)(4,1)S(1)}, u32[]{:S(2)}) copy-start(pred[6]{0:T(512)(128)(4,1)S(1)} %get-tuple-element.84) | copy-start | bytes 22
  15.9 456.4 %copy-start.24 = (pred[3]{0:T(512)(128)(4,1)}, pred[3]{0:T(512)(128)(4,1)S(1)}, u32[]{:S(2)}) copy-start(pred[3]{0:T(512)(128)(4,1)S(1)} %compare_and_fusion) | copy-start | bytes 13
  159.1 2.2 copy-start.8
  160.5 431.8 %all-reduce.13.cloned.1.call-start = ((), (), s32[]{:S(2)}) async-start(), calls=%async_computation.2 | async-start | bytes 393216 | tf_op jit(solution)/shard_map/psum | solution.py:14
  160.6 313.2 %copy-start.17 = (s32[1024]{0:T(1024)}, s32[1024]{0:T(1024)S(1)}, u32[]{:S(2)}) copy-start(s32[1024]{0:T(1024)S(1)} %pad_clamp_fusion) | copy-start | bytes 12292
  473.0 239.9 %all-reduce.15.cloned.1.call-start = ((), (), s32[]{:S(2)}) async-start(), calls=%async_computation.3 | async-start | bytes 131072 | tf_op jit(solution)/shard_map/psum | solution.py:14
  473.8 121.7 %copy-start.13 = (s32[6,1,128]{2,1,0:T(1,128)S(1)}, s32[6,1,128]{2,1,0:T(1,128)}, u32[]{:S(2)}) copy-start(s32[6,1,128]{2,1,0:T(1,128)} %param.20) | copy-start | bytes 9220
  594.6 143.4 %copy-start.23 = (pred[6]{0:T(512)(128)(4,1)S(1)}, pred[6]{0:T(512)(128)(4,1)}, u32[]{:S(2)}) copy-start(pred[6]{0:T(512)(128)(4,1)} %get-tuple-element.83) | copy-start | bytes 22
  594.6 143.4 %copy-start.28 = (pred[6]{0:T(512)(128)(4,1)S(1)}, pred[6]{0:T(512)(128)(4,1)}, u32[]{:S(2)}) copy-start(pred[6]{0:T(512)(128)(4,1)} %copy-done.27) | copy-start | bytes 22
  595.2 454.2 %all-reduce.17.cloned.1.call-start = ((), (), s32[]{:S(2)}) async-start(), calls=%async_computation.4 | async-start | bytes 786432 | tf_op jit(solution)/shard_map/psum | solution.py:14
  597.2 142.2 %copy-start.5 = (f32[3,128,128]{1,2,0:T(8,128)S(1)}, f32[3,128,128]{1,2,0:T(8,128)}, u32[]{:S(2)}) copy-start(f32[3,128,128]{1,2,0:T(8,128)} %all-reduce.13.cloned.1.call-done) | copy-start | bytes 589828
  737.9 1.4 copy-start.10
  738.0 313.2 %copy-start.25 = (pred[3]{0:T(512)(128)(4,1)S(1)}, pred[3]{0:T(512)(128)(4,1)}, u32[]{:S(2)}) copy-start(pred[3]{0:T(512)(128)(4,1)} %copy-done.24) | copy-start | bytes 13
  739.3 312.7 %copy-start.2 = (f32[6,128,128]{1,2,0:T(8,128)S(1)}, f32[6,128,128]{1,2,0:T(8,128)}, u32[]{:S(2)}) copy-start(f32[6,128,128]{1,2,0:T(8,128)} %all-reduce.11.cloned.1.call-done) | copy-start | bytes 1179652
  739.3 431.8 %all-reduce.19.cloned.1.call-start = ((), (), s32[]{:S(2)}) async-start(), calls=%async_computation.5 | async-start | bytes 393216 | tf_op jit(solution)/shard_map/psum | solution.py:14
  740.2 430.9 %copy-start.19 = (pred[3]{0:T(512)(128)(4,1)S(1)}, pred[3]{0:T(512)(128)(4,1)}, u32[]{:S(2)}) copy-start(pred[3]{0:T(512)(128)(4,1)} %copy-done.18) | copy-start | bytes 13
  740.2 430.9 %copy-start.22 = (pred[6,3]{1,0:T(8,128)(4,1)S(1)}, pred[6,3]{1,0:T(8,128)(4,1)}, u32[]{:S(2)}) copy-start(pred[6,3]{1,0:T(8,128)(4,1)} %broadcast_and_fusion) | copy-start | bytes 58
  1049.4 121.7 %copy-start = (f32[6,128,128]{1,2,0:T(8,128)S(1)}, f32[6,128,128]{1,2,0:T(8,128)}, u32[]{:S(2)}) copy-start(f32[6,128,128]{1,2,0:T(8,128)} %all-reduce.17.cloned.1.call-done) | copy-start | bytes 1179652
  1173.3 0.7 copy-start.15
  1174.1 0.7 copy-start.14
  1174.3 1.6 copy-start.16
  1174.3 31.7 %copy-start.9 = (f32[128,128]{1,0:T(8,128)S(1)}, f32[128,128]{1,0:T(8,128)}, u32[]{:S(2)}) copy-start(f32[128,128]{1,0:T(8,128)} %copy-done.8) | copy-start | bytes 196612
  1174.3 115.7 %copy-start.6 = (f32[3,128,128]{1,2,0:T(8,128)S(1)}, f32[3,128,128]{1,2,0:T(8,128)}, u32[]{:S(2)}) copy-start(f32[3,128,128]{1,2,0:T(8,128)} %all-reduce.13.cloned.1.call-done) | copy-start | bytes 589828
  1174.3 115.9 %copy-start.21 = (pred[3]{0:T(512)(128)(4,1)S(1)}, pred[3]{0:T(512)(128)(4,1)}, u32[]{:S(2)}) copy-start(pred[3]{0:T(512)(128)(4,1)} %copy-done.20) | copy-start | bytes 13
  1174.3 116.0 %copy-start.11 = (f32[128,128]{1,0:T(8,128)S(1)}, f32[128,128]{1,0:T(8,128)}, u32[]{:S(2)}) copy-start(f32[128,128]{1,0:T(8,128)} %copy-done.10) | copy-start | bytes 196612
  1291.2 2.7 copy-start.4
  1291.2 3.0 copy-start.26
  1291.3 83.5 %copy-start.3 = (f32[6,128,128]{1,2,0:T(8,128)S(1)}, f32[6,128,128]{1,2,0:T(8,128)}, u32[]{:S(2)}) copy-start(f32[6,128,128]{1,2,0:T(8,128)} %all-reduce.11.cloned.1.call-done) | copy-start | bytes 1179652
  1291.3 83.8 %copy-start.1 = (f32[6,128,128]{1,2,0:T(8,128)S(1)}, f32[6,128,128]{1,2,0:T(8,128)}, u32[]{:S(2)}) copy-start(f32[6,128,128]{1,2,0:T(8,128)} %all-reduce.17.cloned.1.call-done) | copy-start | bytes 1179652
Sparse Core Ops, SparseCore 0:
  14.6 119.4 all-reduce.8
  160.6 310.0 all-reduce.10
  474.2 118.0 all-reduce.12
  595.8 117.0 all-reduce.14
  739.4 309.9 all-reduce.16
  1053.0 118.0 all-reduce.18
where the time goes:
time: 1380 us
  waiting for transfers between devices  1090 us (79%)
  blocking collectives  193 us (14%)
  other arithmetic  57.3 us (4%)
  matrix products  15.1 us (1%)
  between operations  14.7 us (1%)
    psum x6, waiting for transfers between devices, broadcast(): return lax.psum(block, axis)  1090 us
    psum x2, blocking collectives, broadcast(): return lax.psum(block, axis)  163 us
    psum x1, blocking collectives, local(): lax.psum(jnp.einsum('ia,iajc->jc', row_weights, blocks, precision=precise...  30 us
  transfers between devices with their start and end apart: 6, of which 6 were waited for; matrix products, arithmetic and copies ran while one was open for 0% of the time, Pallas kernels for 0%

commit v1 on v0

v1 whole, which is shorter than its diff:
```python
import jax
import jax.numpy as jnp
from jax import lax
from jax.sharding import PartitionSpec as P

precise = lax.Precision.HIGHEST


def dot(spec, a, b):
    return jnp.einsum(spec, a, b, precision=precise)


def factor_tile(tile):
    factor = jnp.linalg.cholesky(tile)
    identity = jnp.eye(tile.shape[0], dtype=jnp.float32)
    inverse = jax.scipy.linalg.solve_triangular(factor, identity, lower=True)
    return factor, inverse


def exchange(message, axis):
    return lax.all_to_all(message, axis, 0, 0, tiled=True)


def everyone(part, count):
    return jnp.broadcast_to(part[None], (count,) + part.shape)


def local(matrix, row_codes, col_codes, fault_tiles, fault_cells, fault_bits):
    grid_rows = lax.axis_size("prow")
    grid_cols = lax.axis_size("pcol")
    grid_row = lax.axis_index("prow")
    grid_col = lax.axis_index("pcol")
    rows, _, size, cols, _, _ = matrix.shape
    share = size // grid_rows
    fold = grid_cols // grid_rows
    blocks = matrix.reshape(rows, size, cols, size)
    row_weights = row_codes.reshape(rows, size).astype(jnp.float32) * 0.25
    col_weights = col_codes.reshape(cols, size).astype(jnp.float32) * 0.25
    tile_row = jnp.arange(rows, dtype=jnp.int32) * grid_rows + grid_row
    tile_col = jnp.arange(cols, dtype=jnp.int32) * grid_cols + grid_col

    magnitude = jnp.exp2(fault_bits.astype(jnp.float32) - 1.0)
    fault_rows = fault_tiles[:, 0] * size + fault_cells[:, 0]
    fault_cols = fault_tiles[:, 1] * size + fault_cells[:, 1]
    offsets = jnp.arange(size, dtype=jnp.int32)
    local_rows = (tile_row[:, None] * size + offsets[None, :]).reshape(-1)
    local_cols = (tile_col[:, None] * size + offsets[None, :]).reshape(-1)
    hit_rows = (fault_rows[:, None] == local_rows[None, :]).astype(jnp.float32) * magnitude[:, None]
    hit_cols = (fault_cols[:, None] == local_cols[None, :]).astype(jnp.float32)
    faults_added = dot("fr,fc->rc", hit_rows, hit_cols).reshape(rows, size, cols, size)
    mirror_rows = (fault_cols[:, None] == local_rows[None, :size]).astype(jnp.float32)
    mirror_cols = (fault_rows[:, None] == local_cols[None, :]).astype(jnp.float32) * magnitude[:, None]
    mirrored = dot("fr,fc->rc", mirror_rows, mirror_cols).reshape(size, cols, size)

    col_part = dot("ia,iajc->jc", row_weights, blocks)
    row_part = dot("iajc,jc->ia", blocks, col_weights)
    strip = blocks[0] + mirrored
    below = jnp.where((tile_col > grid_row)[:, None], col_weights, 0.0)
    panel_part = dot("ajc,jc->a", strip, below)[None]

    pieces = strip.reshape(grid_rows, share, cols, size).transpose(0, 2, 1, 3)
    message = jnp.concatenate(
        [
            pieces.reshape(grid_rows, cols * share, size),
            everyone(jnp.concatenate([col_part, panel_part]), grid_rows),
        ],
        axis=1,
    )
    first = exchange(message, "prow")
    own_share = first[:2, : cols * share].reshape(2 * cols * share, size)
    col_check = jnp.sum(first[:, cols * share : cols * share + cols], axis=0)
    panel_part = first[:2, cols * share + cols]

    message = jnp.concatenate([own_share, row_part, panel_part, col_check[:1], col_weights[:1]])
    second = exchange(everyone(message, grid_cols), "pcol")
    depth = 2 * cols * share
    shares = second[:, :depth]
    row_check = jnp.sum(second[:, depth : depth + rows], axis=0)
    panel_sum = jnp.sum(second[:, depth + rows : depth + rows + 2], axis=0)
    check_0, check_1 = second[0, depth + rows + 2], second[1, depth + rows + 2]
    weight_0, weight_1 = second[0, depth + rows + 3], second[1, depth + rows + 3]

    by_row = shares.reshape(fold, grid_rows, depth, size).transpose(1, 0, 2, 3)
    corner = jnp.concatenate(
        [shares[0, :share], shares[1, :share], shares[1, cols * share : cols * share + share]]
    )
    message = jnp.concatenate(
        [
            by_row.reshape(grid_rows, fold * depth, size),
            everyone(jnp.concatenate([own_share, corner]), grid_rows),
        ],
        axis=1,
    )
    third = exchange(message, "prow")
    row_panel = third[:, : fold * depth].reshape(grid_rows, fold, 2, cols, share, size)
    row_panel = row_panel.transpose(2, 0, 4, 3, 1, 5).reshape(2, size, rows, size)
    col_panel = third[:, fold * depth : (fold + 1) * depth].reshape(grid_rows, 2, cols, share, size)
    col_panel = col_panel.transpose(1, 0, 3, 2, 4).reshape(2, size, cols, size)
    corner = third[:, (fold + 1) * depth :].reshape(grid_rows, 3, share, size)
    corner = corner.transpose(1, 0, 2, 3).reshape(3, size, size)

    factor_0, inverse_0 = factor_tile(corner[0])
    below_0 = dot("ab,bc->ac", inverse_0, corner[1])
    factor_1, inverse_1 = factor_tile(corner[2] - dot("ba,bc->ac", below_0, below_0))
    mixed = -dot("ab,bc->ac", inverse_1, dot("ba,bc->ac", below_0, inverse_0))
    transform = jnp.concatenate(
        [
            jnp.concatenate([inverse_0, jnp.zeros_like(inverse_0)], axis=1),
            jnp.concatenate([mixed, inverse_1], axis=1),
        ]
    )
    factors = jnp.stack([factor_0.T, factor_1.T])

    steps = jnp.arange(2, dtype=jnp.int32)

    def panels(raw, tiles):
        product = dot("ab,bc->ac", transform, raw.reshape(2 * size, -1))
        product = product.reshape(2, size, tiles.shape[0], size)
        after = (tiles[None, :] > steps[:, None])[:, None, :, None]
        level = (tiles[None, :] == steps[:, None])[:, None, :, None]
        trailing = jnp.where(after, product, 0.0)
        return trailing, jnp.where(level, factors[:, :, None, :], trailing)

    row_trailing, row_full = panels(row_panel, tile_row)
    col_trailing, _ = panels(col_panel, tile_col)

    new_0 = dot("ab,b->a", inverse_0, check_0)
    new_1 = dot("ab,b->a", inverse_1, check_1 - dot("ba,b->a", below_0, new_0))
    shift_0 = dot("ab,b->a", inverse_0, panel_sum[0]) + dot("ba,b->a", factor_0, weight_0) - weight_0
    rest = dot("ab,b->a", inverse_0, panel_sum[0] - dot("ab,b->a", corner[1], weight_1))
    shift_1 = dot("ab,b->a", inverse_1, panel_sum[1] - dot("ba,b->a", below_0, rest))
    shift_1 = shift_1 + dot("ba,b->a", factor_1, weight_1) - weight_1
    new = jnp.stack([new_0, new_1])
    shift = jnp.stack([shift_0, shift_1])
    row_check = row_check - dot("kbia,kb->ia", row_full, shift)
    col_check = col_check - dot("kbja,kb->ja", col_trailing, new)
    col_check = jnp.where((tile_col == 0)[:, None], new_0, col_check)
    col_check = jnp.where((tile_col == 1)[:, None], new_1, col_check)

    update = dot(
        "br,bc->rc",
        row_trailing.reshape(2 * size, rows * size),
        col_trailing.reshape(2 * size, cols * size),
    )
    blocks = blocks + faults_added - update.reshape(rows, size, cols, size)
    settled = jnp.where(grid_col == 0, row_full[0], row_full[1]).transpose(1, 2, 0)
    blocks = jnp.concatenate(
        [jnp.where(grid_col < 2, settled, blocks[:, :, 0])[:, :, None], blocks[:, :, 1:]], axis=2
    )
    cleared = (tile_row < 2)[:, None] & (tile_col[None, :] > tile_row[:, None])
    blocks = jnp.where(cleared[:, None, :, None], 0.0, blocks)

    col_part = dot("ia,iajc->jc", row_weights, blocks)
    row_part = dot("iajc,jc->ia", blocks, col_weights)
    col_found = jnp.sum(exchange(everyone(col_part, grid_rows), "prow"), axis=0)
    row_found = jnp.sum(exchange(everyone(row_part, grid_cols), "pcol"), axis=0)
    col_flags = jnp.max(jnp.abs(col_check - col_found), axis=1)
    row_flags = jnp.max(jnp.abs(row_check - row_found), axis=1)
    return (
        blocks.reshape(matrix.shape),
        col_check.reshape(cols, 1, size),
        row_check.reshape(rows, 1, size),
        col_flags.reshape(cols, 1),
        row_flags.reshape(rows, 1),
    )


def solution(mesh):
    return jax.shard_map(
        local,
        mesh=mesh,
        in_specs=(
            P(None, "prow", None, None, "pcol", None),
            P(None, "prow", None),
            P(None, "pcol", None),
            P(),
            P(),
            P(),
        ),
        out_specs=(
            P(None, "prow", None, None, "pcol", None),
            P(None, "pcol", None),
            P(None, "prow", None),
            P(None, "pcol"),
            P(None, "prow"),
        ),
        check_vma=False,
    )
```

time: 1380 us -> 199 us (0.14)
  the two profiles are of different devices: /device:TPU:64 before, /device:TPU:1 now
where the time goes in v1:
time: 199 us; the launch traced here: 198 us
  other arithmetic  55.8 us (28%)
  blocking collectives  37.5 us (19%)
  starting transfers between devices  29.7 us (15%)
  waiting for transfers between devices  29 us (15%)
  local copies, waits for them, and re-layouts  23.6 us (12%)
  matrix products  20.9 us (11%)
    all_to_all x1, blocking collectives, exchange(): return lax.all_to_all(message, axis, 0, 0, tiled=True)  37.5 us
    all_to_all x4, starting transfers between devices, exchange(): return lax.all_to_all(message, axis, 0, 0, tiled=True)  29.7 us
    all_to_all x4, waiting for transfers between devices, exchange(): return lax.all_to_all(message, axis, 0, 0, tiled=True)  29 us
    another operation x6, other arithmetic, factor_tile(): factor = jnp.linalg.cholesky(tile)  24.8 us
    dot_general x26, matrix products, dot(): return jnp.einsum(spec, a, b, precision=precise)  20.4 us
    another operation x2, other arithmetic, factor_tile(): inverse = jax.scipy.linalg.solve_triangular(factor, identity, lower=True)  19.8 us
    unnamed x76, local copies, waits for them, and re-layouts  12.2 us
  transfers between devices with their start and end apart: 4, of which 4 were waited for; matrix products, arithmetic and copies ran while one was open for 7% of the time, Pallas kernels for 0%

profile of v1, /device:TPU:1, one launch (start us, length us, event | category | flops | bytes accessed | tf_op | source)
XLA Modules:
  0.0 197.9 jit_solution(7752582850793526890)
XLA Ops:
  0.6 0.5 multiply_add_fusion.1
  1.7 1.0 slice.120
  2.7 3.4 %copy.105 = f32[6,1,128,3,1,128]{2,5,0,3,4,1:T(8,128)S(1)} copy(f32[6,1,128,3,1,128]{5,4,3,2,1,0:T(1,128)} %param.9) | data formatting | bytes 2359296 | tf_op args[0]
  6.4 0.5 copy-done.12
  7.6 1.1 fusion.2
  9.2 0.7 pad_maximum_fusion.1
  9.9 10.8 %all-to-all-start = ((f32[16,28,128]{2,1,0:T(8,128)}), f32[16,28,128]{2,1,0:T(8,128)}, u32[]{:S(2)}, u32[]{:S(2)}) async-start(f32[16,28,128]{2,1,0:T(8,128)} %pad_maximum_fusion.1), calls=%async_computation | async-start | bytes 524288 | tf_op jit(solution)/shard_map/all_to_all | solution.py:21
  20.7 0.9 copy.150
  21.6 0.7 fusion
  22.3 5.7 %all-to-all-done = f32[16,28,128]{2,1,0:T(8,128)} async-done(((f32[16,28,128]{2,1,0:T(8,128)}), f32[16,28,128]{2,1,0:T(8,128)}, u32[]{:S(2)}, u32[]{:S(2)}) %all-to-all-start) | async-done | bytes 229408 | tf_op jit(solution)/shard_map/all_to_all | solution.py:21
  28.0 0.9 slice_reduce_fusion.2
  28.9 0.7 slice.155
  29.6 0.7 slice.154
  30.5 37.5 %all_to_all.25 = f32[32,58,128]{2,1,0:T(8,128)S(1)} all-to-all(f32[32,58,128]{2,1,0:T(8,128)S(1)} %broadcast_in_dim.161), channel_id=1, replica_groups=mesh['prow'=16,'pcol'=32] {'pcol'}, dimensions={0} | all-to-all | bytes 1900544 | tf_op jit(solution)/shard_map/all_to_all | solution.py:21
  68.1 0.9 copy-done.2
  69.0 1.2 pad_maximum_fusion
  70.2 7.6 %all-to-all-start.2 = ((f32[16,168,128]{2,1,0:T(8,128)}), f32[16,168,128]{2,1,0:T(8,128)S(1)}, u32[]{:S(2)}, u32[]{:S(2)}) async-start(f32[16,168,128]{2,1,0:T(8,128)} %pad_maximum_fusion), calls=%async_computation.2 | async-start | bytes 2752512 | tf_op jit(solution)/shard_map/all_to_all | solution.py:21
  77.9 1.7 fusion.24
  79.6 2.5 %reshape.311 = f32[6,128,3,128]{1,0,3,2:T(8,128)} reshape(f32[768,384]{0,1:T(8,128)} %fusion.24) | data formatting | bytes 2359296 | tf_op jit(solution)/shard_map/reshape | solution.py:50
  82.1 0.6 broadcast_compare_fusion
  82.8 0.5 iota_compare_fusion.7
  83.3 0.6 compare_and_fusion
  83.9 0.9 slice_reduce_fusion
  84.8 0.9 slice_reduce_fusion.1
  85.7 11.6 %all-to-all-done.2 = f32[16,168,128]{2,1,0:T(8,128)S(1)} async-done(((f32[16,168,128]{2,1,0:T(8,128)}), f32[16,168,128]{2,1,0:T(8,128)S(1)}, u32[]{:S(2)}, u32[]{:S(2)}) %all-to-all-start.2) | async-done | bytes 1376288 | tf_op jit(solution)/shard_map/all_to_all | solution.py:21
  97.6 11.7 %cholesky.44 = f32[128,128]{1,0:T(8,128)S(1)} custom-call(f32[128,128]{1,0:T(8,128)S(1)} %fusion.50), custom_call_target="Cholesky" | custom-call | tf_op jit(solution)/shard_map/jit(cholesky)/cholesky | solution.py:14
  109.4 0.6 compare_reduce_fusion.1
  110.0 0.7 fusion.53
  110.7 9.8 %custom-call.6 = f32[1,128,128]{1,2,0:T(8,128)S(1)} custom-call(f32[1,128,128]{2,1,0:T(8,128)S(1)} %get-tuple-element.42), custom_call_target="InvertDiagBlocksLowerTriangular" | custom-call | tf_op jit(solution)/shard_map/jit(_solve_triangular)/triangular_solve | solution.py:16
  121.6 0.8 convolution_bitcast_fusion.6
  122.4 0.8 fusion.8
  123.8 11.7 %cholesky.55 = f32[128,128]{1,0:T(8,128)S(1)} custom-call(f32[128,128]{1,0:T(8,128)S(1)} %fusion.48), custom_call_target="Cholesky" | custom-call | tf_op jit(solution)/shard_map/jit(cholesky)/cholesky | solution.py:14
  135.5 0.6 compare_reduce_fusion
  136.2 0.7 fusion.54
  136.9 0.7 copy.113
  137.6 10.0 %custom-call.7 = f32[1,128,128]{1,2,0:T(8,128)S(1)} custom-call(f32[1,128,128]{2,1,0:T(8,128)S(1)} %get-tuple-element.44), custom_call_target="InvertDiagBlocksLowerTriangular" | custom-call | tf_op jit(solution)/shard_map/jit(_solve_triangular)/triangular_solve | solution.py:16
  148.0 0.9 fusion.75
  148.8 0.9 fusion.11
  149.9 0.7 convolution_bitcast_fusion.1
  150.9 0.6 pad_maximum_fusion.5
  151.6 1.1 copy.117
  153.0 0.6 convolution_select_fusion.1
  154.2 0.9 copy.184
  155.1 1.8 broadcast_select_fusion
  156.9 0.5 copy.120
  157.5 1.3 copy-done.1
  158.8 2.3 %convolution_subtract_fusion = f32[6,128,3,128]{1,3,0,2:T(8,128)S(1)} fusion(f32[6,128,256,1]{2,1,0,3:T(8,128)S(1)} %bitcast.332, f32[3,128,256,1]{2,1,3,0:T(8,128)} %bitcast.344, f32[6,1,128,3,1,128]{2,5,0,3,4,1:T(8,128)S(1)} %copy.105, f32[6,128,3,128]{1,0,3,2:T(8,128)S(1)} %copy-done.1), kind=kOutput, calls=%fused_computation | convolution fusion | flops 906559488 | bytes 4718592 | tf_op jit(solution)/shard_map/br,bc->rc/dot_general | solution.py:10
  161.3 0.6 copy-done.7
  161.9 1.6 fusion.13
  163.5 1.6 fusion.15
  165.8 1.1 fusion.17
  166.9 0.7 broadcast_in_dim.175
  167.6 4.3 %all-to-all-start.3 = ((f32[16,3,128]{2,1,0:T(4,128)}), f32[16,3,128]{2,1,0:T(4,128)S(1)}, u32[]{:S(2)}, u32[]{:S(2)}) async-start(f32[16,3,128]{2,1,0:T(4,128)} %broadcast_in_dim.175), calls=%async_computation.3 | async-start | bytes 65536 | tf_op jit(solution)/shard_map/all_to_all | solution.py:21
  172.0 0.5 copy-done.11
  172.5 0.8 fusion.16
  173.4 2.6 %copy.128 = f32[6,1,128,3,1,128]{5,4,3,2,1,0:T(1,128)} copy(f32[6,1,128,3,1,128]{2,5,0,3,4,1:T(8,128)S(1)} %maximum_select_fusion) | data formatting | bytes 2359296
  176.0 1.6 all-to-all-done.3
  177.6 0.7 broadcast_in_dim.176
  178.3 7.0 %all-to-all-start.4 = ((f32[32,6,128]{2,1,0:T(8,128)}), f32[32,6,128]{2,1,0:T(8,128)S(1)}, u32[]{:S(2)}, u32[]{:S(2)}) async-start(f32[32,6,128]{2,1,0:T(8,128)} %broadcast_in_dim.176), calls=%async_computation.4 | async-start | bytes 262144 | tf_op jit(solution)/shard_map/all_to_all | solution.py:21
  185.4 0.7 abs_reduce_fusion.1
  186.1 0.6 copy.129
  186.6 10.0 %all-to-all-done.4 = f32[32,6,128]{2,1,0:T(8,128)S(1)} async-done(((f32[32,6,128]{2,1,0:T(8,128)}), f32[32,6,128]{2,1,0:T(8,128)S(1)}, u32[]{:S(2)}, u32[]{:S(2)}) %all-to-all-start.4) | async-done | bytes 98336 | tf_op jit(solution)/shard_map/all_to_all | solution.py:21
  196.7 0.6 abs_reduce_fusion
  197.3 0.6 copy.130
  (132 shorter events, 7.0 us)
Async XLA Ops:
  2.7 3.4 %copy-start.34 = (s32[96]{0:T(128)S(1)}, s32[96]{0:T(128)}, u32[]{:S(2)}) copy-start(s32[96]{0:T(128)} %param.14) | copy-start | bytes 1156
  2.7 3.6 %copy-start.10 = (s32[3,1,128]{2,1,0:T(1,128)S(1)}, s32[3,1,128]{2,1,0:T(1,128)}, u32[]{:S(2)}) copy-start(s32[3,1,128]{2,1,0:T(1,128)} %param.11) | copy-start | bytes 4612
  2.7 3.6 %copy-start.24 = (s32[96,2]{0,1:T(2,128)S(1)}, s32[96,2]{0,1:T(2,128)}, u32[]{:S(2)}) copy-start(s32[96,2]{0,1:T(2,128)} %param.13) | copy-start | bytes 2308
  2.7 3.6 %copy-start.25 = (s32[96,2]{0,1:T(2,128)S(1)}, s32[96,2]{0,1:T(2,128)}, u32[]{:S(2)}) copy-start(s32[96,2]{0,1:T(2,128)} %param.12) | copy-start | bytes 2308
  6.1 1.4 copy-start.19
  6.2 1.3 copy-start.21
  6.4 0.6 copy-start.12
  6.4 0.6 copy-start.14
  7.6 13.1 %copy-start = (f32[6,1,128,3,1,128]{5,4,3,2,1,0:T(1,128)S(1)}, f32[6,1,128,3,1,128]{5,4,3,2,1,0:T(1,128)}, u32[]{:S(2)}) copy-start(f32[6,1,128,3,1,128]{5,4,3,2,1,0:T(1,128)} %param.9) | copy-start | bytes 3538948
  9.9 18.1 %all-to-all-start = ((f32[16,28,128]{2,1,0:T(8,128)}), f32[16,28,128]{2,1,0:T(8,128)}, u32[]{:S(2)}, u32[]{:S(2)}) async-start(f32[16,28,128]{2,1,0:T(8,128)} %pad_maximum_fusion.1), calls=%async_computation | async-start | bytes 524288 | tf_op jit(solution)/shard_map/all_to_all | solution.py:21
  68.0 1.0 copy-start.2
  70.2 7.6 %copy-start.13 = (s32[96]{0:T(128)S(1)}, s32[96]{0:T(128)}, u32[]{:S(2)}) copy-start(s32[96]{0:T(128)} %copy-done.12) | copy-start | bytes 1156
  70.2 7.6 %copy-start.15 = (s32[96]{0:T(128)S(1)}, s32[96]{0:T(128)}, u32[]{:S(2)}) copy-start(s32[96]{0:T(128)} %copy-done.14) | copy-start | bytes 1156
  70.2 7.7 %copy-start.22 = (f32[96]{0:T(128)S(1)}, f32[96]{0:T(128)}, u32[]{:S(2)}) copy-start(f32[96]{0:T(128)} %copy-done.21) | copy-start | bytes 1156
  70.2 27.1 %all-to-all-start.2 = ((f32[16,168,128]{2,1,0:T(8,128)}), f32[16,168,128]{2,1,0:T(8,128)S(1)}, u32[]{:S(2)}, u32[]{:S(2)}) async-start(f32[16,168,128]{2,1,0:T(8,128)} %pad_maximum_fusion), calls=%async_computation.2 | async-start | bytes 2752512 | tf_op jit(solution)/shard_map/all_to_all | solution.py:21
  79.6 3.1 %copy-start.33 = (s32[3]{0:T(128)S(1)}, s32[3]{0:T(128)}, u32[]{:S(2)}) copy-start(s32[3]{0:T(128)} %get-tuple-element.55) | copy-start | bytes 40
  79.6 3.1 %copy-start.32 = (s32[6]{0:T(128)S(1)}, s32[6]{0:T(128)}, u32[]{:S(2)}) copy-start(s32[6]{0:T(128)} %get-tuple-element.59) | copy-start | bytes 76
  109.3 1.4 copy-start.6
  135.5 1.4 copy-start.8
  149.9 1.7 copy-start.16
  153.0 0.9 copy-start.18
  153.0 2.0 %copy-start.4 = (f32[256,256]{1,0:T(8,128)}, f32[256,256]{1,0:T(8,128)S(1)}, u32[]{:S(2)}) copy-start(f32[256,256]{1,0:T(8,128)S(1)} %select_maximum_fusion) | copy-start | bytes 786436
  153.6 1.4 copy-start.3
  153.9 1.2 copy-start.5
  153.9 1.2 copy-start.26
  153.9 1.2 copy-start.27
  157.4 1.4 copy-start.1
  161.1 0.8 copy-start.7
  161.1 0.8 copy-start.28
  161.1 2.4 %copy-start.9 = (f32[128,128]{1,0:T(8,128)S(1)}, f32[128,128]{1,0:T(8,128)}, u32[]{:S(2)}) copy-start(f32[128,128]{1,0:T(8,128)} %copy-done.8) | copy-start | bytes 196612
  161.1 2.4 %copy-start.29 = (f32[128]{0:T(128)S(1)}, f32[128]{0:T(128)}, u32[]{:S(2)}) copy-start(f32[128]{0:T(128)} %convolution_bitcast_fusion.1) | copy-start | bytes 1540
  165.1 0.7 copy-start.20
  165.1 0.7 copy-start.23
  167.6 10.1 %all-to-all-start.3 = ((f32[16,3,128]{2,1,0:T(4,128)}), f32[16,3,128]{2,1,0:T(4,128)S(1)}, u32[]{:S(2)}, u32[]{:S(2)}) async-start(f32[16,3,128]{2,1,0:T(4,128)} %broadcast_in_dim.175), calls=%async_computation.3 | async-start | bytes 65536 | tf_op jit(solution)/shard_map/all_to_all | solution.py:21
  171.8 0.7 copy-start.11
  173.3 12.0 %copy-start.17 = (f32[1,128]{1,0:T(1,128)S(1)}, f32[1,128]{1,0:T(1,128)}, u32[]{:S(2)}) copy-start(f32[1,128]{1,0:T(1,128)} %copy-done.16) | copy-start | bytes 1540
  173.3 12.0 %copy-start.30 = (pred[3]{0:T(512)(128)(4,1)S(1)}, pred[3]{0:T(512)(128)(4,1)}, u32[]{:S(2)}) copy-start(pred[3]{0:T(512)(128)(4,1)} %get-tuple-element.57) | copy-start | bytes 13
  173.3 12.0 %copy-start.31 = (pred[3]{0:T(512)(128)(4,1)S(1)}, pred[3]{0:T(512)(128)(4,1)}, u32[]{:S(2)}) copy-start(pred[3]{0:T(512)(128)(4,1)} %get-tuple-element.58) | copy-start | bytes 13
  178.3 18.3 %all-to-all-start.4 = ((f32[32,6,128]{2,1,0:T(8,128)}), f32[32,6,128]{2,1,0:T(8,128)S(1)}, u32[]{:S(2)}, u32[]{:S(2)}) async-start(f32[32,6,128]{2,1,0:T(8,128)} %broadcast_in_dim.176), calls=%async_computation.4 | async-start | bytes 262144 | tf_op jit(solution)/shard_map/all_to_all | solution.py:21

commit v2 on v1

v2 whole, which is shorter than its diff:
```python
import functools

import jax
import jax.numpy as jnp
from jax import lax
from jax.experimental import pallas as pl
from jax.experimental.pallas import tpu as pltpu
from jax.sharding import PartitionSpec as P

SIZE = 128
GROUP = 8
precise = lax.Precision.HIGHEST
VMEM = pl.BlockSpec(memory_space=pltpu.VMEM)
SMEM = pl.BlockSpec(memory_space=pltpu.SMEM)


def exchange(message, axis):
    return lax.all_to_all(message, axis, 0, 0, tiled=True)


def everyone(part, count):
    return jnp.broadcast_to(part[None], (count,) + part.shape)


def mm(a, b):
    return jnp.dot(a, b, precision=precise, preferred_element_type=jnp.float32)


def mm_nt(a, b):
    return lax.dot_general(
        a, b, (((1,), (1,)), ((), ())), precision=precise, preferred_element_type=jnp.float32
    )


def factor_tile(tile):
    lanes = lambda v, c: jnp.broadcast_to(v[:, c : c + 1], v.shape)
    rows = lambda v, j: jnp.broadcast_to(v[j : j + 1, :], v.shape)
    groups = SIZE // GROUP
    sub = lax.broadcasted_iota(jnp.int32, (GROUP, SIZE), 0)
    lan = lax.broadcasted_iota(jnp.int32, (GROUP, SIZE), 1)
    left = [tile[GROUP * i : GROUP * (i + 1), :] for i in range(groups)]
    right = [jnp.where(lan == sub + GROUP * i, 1.0, 0.0) for i in range(groups)]
    upper, inverse = [], []
    for b in range(groups):
        first = GROUP * b
        column = [lanes(left[b], first + j) for j in range(GROUP)]
        d = [[rows(column[j], i) if j <= i else None for j in range(GROUP)] for i in range(GROUP)]
        ra = [rows(left[b], j) for j in range(GROUP)]
        rb = [rows(right[b], j) for j in range(GROUP)]
        scale = []
        for k in range(GROUP):
            scale.append(lax.rsqrt(d[k][k]))
            for i in range(k + 1, GROUP):
                d[i][k] = d[i][k] * scale[k]
            for j in range(k + 1, GROUP):
                for i in range(j, GROUP):
                    d[i][j] = d[i][j] - d[i][k] * d[j][k]
        for j in range(GROUP):
            for k in range(j):
                ra[j] = ra[j] - d[j][k] * ra[k]
                rb[j] = rb[j] - d[j][k] * rb[k]
            ra[j] = ra[j] * scale[j]
            rb[j] = rb[j] * scale[j]
        for i in range(b + 1, groups):
            c = [lanes(left[i], first + j) for j in range(GROUP)]
            for j in range(GROUP):
                for k in range(j):
                    c[j] = c[j] - d[j][k] * c[k]
                c[j] = c[j] * scale[j]
            for j in range(GROUP):
                left[i] = left[i] - c[j] * ra[j]
                right[i] = right[i] - c[j] * rb[j]
        out_a, out_b = ra[GROUP - 1], rb[GROUP - 1]
        for j in range(GROUP - 1):
            out_a = jnp.where(sub == j, ra[j], out_a)
            out_b = jnp.where(sub == j, rb[j], out_b)
        upper.append(jnp.where(lan >= sub + first, out_a, 0.0))
        inverse.append(out_b)
    return jnp.concatenate(upper), jnp.concatenate(inverse)


def columns_of(weights):
    count = weights.shape[0]
    padded = jnp.concatenate([weights, jnp.zeros((SIZE - count, SIZE), jnp.float32)])
    turned = padded.T
    return [jnp.broadcast_to(turned[:, t : t + 1], (SIZE, SIZE)) for t in range(count)]


def hits(fault_row, first, scale=None):
    place = first + lax.broadcasted_iota(jnp.int32, (SIZE, SIZE), 0)
    found = jnp.where(fault_row == place, 1.0 if scale is None else scale, 0.0)
    return found.astype(jnp.bfloat16)


def fault_tile(row_hits, col_hits):
    return lax.dot_general(
        row_hits, col_hits, (((1,), (1,)), ((), ())), preferred_element_type=jnp.float32
    )


def pre_kernel(geometry, place, faults, matrix, row_codes, col_codes, message, row_part):
    rows, cols, grid_rows, grid_cols = geometry
    grid_row, grid_col = place[0], place[1]
    share = SIZE // grid_rows
    row_weights = row_codes[...].astype(jnp.float32) * 0.25
    col_weights = col_codes[...].astype(jnp.float32) * 0.25
    turned = columns_of(row_weights)
    ones = jnp.ones((8, SIZE), jnp.float32)
    fault_row, fault_col = faults[0:1, :], faults[1:2, :]
    magnitude = faults[2:3, :].astype(jnp.float32)
    mirror_rows = hits(fault_col, grid_row * SIZE)
    col_sums = [jnp.zeros((SIZE, SIZE), jnp.float32) for _ in range(cols)]
    panel = jnp.zeros((SIZE, SIZE), jnp.float32)
    for t in range(rows):
        total = jnp.zeros((SIZE, SIZE), jnp.float32)
        for u in range(cols):
            tile = matrix[pl.ds(t * SIZE * cols + u, SIZE, cols), :]
            weight = col_weights[u : u + 1]
            total = total + tile * weight
            col_sums[u] = col_sums[u] + tile * turned[t]
            if t == 0:
                col_tile = u * grid_cols + grid_col
                tile = tile + fault_tile(mirror_rows, hits(fault_row, col_tile * SIZE, magnitude))
                panel = panel + tile * jnp.where(col_tile > grid_row, weight, 0.0)
                for i in range(grid_rows):
                    message[i, u * share : (u + 1) * share, :] = tile[i * share : (i + 1) * share]
        row_part[t : t + 1, :] = mm_nt(ones, total)[0:1]
    row_part[rows:8, :] = jnp.zeros((8 - rows, SIZE), jnp.float32)
    sums = [jnp.sum(col_sums[u], axis=0, keepdims=True) for u in range(cols)]
    sums.append(mm_nt(ones, panel)[0:1])
    sums.append(jnp.zeros((8 - cols - 1, SIZE), jnp.float32))
    sums = jnp.concatenate(sums)
    for i in range(grid_rows):
        message[i, cols * share : cols * share + 8, :] = sums


def post_kernel(
    geometry,
    place,
    faults,
    third,
    vectors,
    row_sums,
    col_sums,
    matrix,
    row_codes,
    col_codes,
    factored,
    col_check,
    row_check,
    col_message,
    row_message,
):
    rows, cols, grid_rows, grid_cols = geometry
    grid_row, grid_col = place[0], place[1]
    share = SIZE // grid_rows
    fold = grid_cols // grid_rows
    depth = 2 * cols * share

    def gathered(start):
        return jnp.concatenate([third[i, start : start + share, :] for i in range(grid_rows)])

    corner = [gathered((fold + 1) * depth + k * share) for k in range(3)]
    tile_0 = (corner[0] + corner[0].T) * 0.5
    upper_0, inverse_0 = factor_tile(tile_0)
    below_0 = mm(inverse_0, corner[1])
    tile_1 = corner[2] - mm(below_0.T, below_0)
    upper_1, inverse_1 = factor_tile((tile_1 + tile_1.T) * 0.5)
    mixed = -mm(inverse_1, mm(below_0.T, inverse_0))
    transform = jnp.concatenate(
        [
            jnp.concatenate([inverse_0, jnp.zeros_like(inverse_0)], axis=1),
            jnp.concatenate([mixed, inverse_1], axis=1),
        ]
    )

    vec = vectors[...]
    check_0, check_1, sum_0, sum_1, weight_0, weight_1 = (vec[i : i + 1] for i in range(6))
    rest = sum_0 - mm_nt(weight_1, corner[1])
    pad = jnp.zeros((5, 2 * SIZE), jnp.float32)
    stacked = jnp.concatenate(
        [
            jnp.concatenate([check_0, check_1], axis=1),
            jnp.concatenate([sum_0, sum_1], axis=1),
            jnp.concatenate([rest, sum_1], axis=1),
            pad,
        ]
    )
    solved = mm_nt(stacked, transform)
    new = solved[0:1]
    shift_0 = solved[1:2, :SIZE] + mm_nt(weight_0, upper_0) - weight_0
    shift_1 = solved[2:3, SIZE:] + mm_nt(weight_1, upper_1) - weight_1
    shift = jnp.concatenate([shift_0, shift_1], axis=1)

    row_weights = row_codes[...].astype(jnp.float32) * 0.25
    col_weights = col_codes[...].astype(jnp.float32) * 0.25
    turned = columns_of(row_weights)
    ones = jnp.ones((8, SIZE), jnp.float32)
    fault_row, fault_col = faults[0:1, :], faults[1:2, :]
    magnitude = faults[2:3, :].astype(jnp.float32)

    zero = jnp.zeros((SIZE, SIZE), jnp.float32)
    col_panels, col_hits = [], []
    for u in range(cols):
        raw = jnp.concatenate(
            [gathered(fold * depth + (k * cols + u) * share) for k in range(2)]
        )
        panel = mm(transform, raw)
        if u == 0:
            panel = jnp.concatenate(
                [
                    jnp.where(grid_col > 0, panel[:SIZE], zero),
                    jnp.where(grid_col > 1, panel[SIZE:], zero),
                ]
            )
        col_panels.append(panel)
        col_hits.append(hits(fault_col, (u * grid_cols + grid_col) * SIZE))
        checked = col_sums[u : u + 1, :] - mm(new, panel)
        if u == 0:
            checked = jnp.where(grid_col == 0, new[:, :SIZE], checked)
            checked = jnp.where(grid_col == 1, new[:, SIZE:], checked)
        col_check[u : u + 1, :] = checked

    found = [jnp.zeros((SIZE, SIZE), jnp.float32) for _ in range(cols)]
    found_rows = []
    for t in range(rows):
        h, j = t % fold, t // fold
        raw = jnp.concatenate([gathered(h * depth + (k * cols + j) * share) for k in range(2)])
        panel = mm(transform, raw)
        full = panel
        if t == 0:
            panel = jnp.concatenate(
                [
                    jnp.where(grid_row > 0, panel[:SIZE], zero),
                    jnp.where(grid_row > 1, panel[SIZE:], zero),
                ]
            )
            full = jnp.concatenate(
                [
                    jnp.where(grid_row == 0, upper_0, panel[:SIZE]),
                    jnp.where(grid_row == 1, upper_1, panel[SIZE:]),
                ]
            )
        row_check[t : t + 1, :] = row_sums[t : t + 1, :] - mm(shift, full)
        upright = panel.T
        row_hits = hits(fault_row, (t * grid_rows + grid_row) * SIZE, magnitude)
        total = jnp.zeros((SIZE, SIZE), jnp.float32)
        for u in range(cols):
            where = pl.ds(t * SIZE * cols + u, SIZE, cols)
            tile = matrix[where, :] + fault_tile(row_hits, col_hits[u]) - mm(upright, col_panels[u])
            if u == 0:
                kept = full.T if t == 0 else upright
                tile = jnp.where(grid_col == 0, kept[:, :SIZE], tile)
                tile = jnp.where(grid_col == 1, kept[:, SIZE:], tile)
            if t == 0:
                cleared = (grid_row < 2) & (u * grid_cols + grid_col > grid_row)
                tile = jnp.where(cleared, zero, tile)
            factored[where, :] = tile
            total = total + tile * col_weights[u : u + 1]
            found[u] = found[u] + tile * turned[t]
        found_rows.append(mm_nt(ones, total)[0:1])
    found_rows.append(jnp.zeros((8 - rows, SIZE), jnp.float32))
    found_rows = jnp.concatenate(found_rows)
    found_cols = [jnp.sum(found[u], axis=0, keepdims=True) for u in range(cols)]
    found_cols.append(jnp.zeros((8 - cols, SIZE), jnp.float32))
    found_cols = jnp.concatenate(found_cols)
    for i in range(grid_rows):
        col_message[i] = found_cols
    for i in range(grid_cols):
        row_message[i] = found_rows


def local(matrix, row_codes, col_codes, fault_tiles, fault_cells, fault_bits):
    grid_rows = lax.axis_size("prow")
    grid_cols = lax.axis_size("pcol")
    grid_row = lax.axis_index("prow")
    grid_col = lax.axis_index("pcol")
    rows, _, size, cols, _, _ = matrix.shape
    share = size // grid_rows
    fold = grid_cols // grid_rows
    depth = 2 * cols * share
    geometry = (rows, cols, grid_rows, grid_cols)
    f32 = lambda *shape: jax.ShapeDtypeStruct(shape, jnp.float32)

    flat = matrix.reshape(rows * size * cols, size)
    row_codes = row_codes.reshape(rows, size)
    col_codes = col_codes.reshape(cols, size)
    place = jnp.stack([grid_row, grid_col]).astype(jnp.int32)
    spots = fault_tiles.T * size + fault_cells.T
    magnitude = jnp.left_shift(1, fault_bits - 1)
    faults = jnp.concatenate([spots, magnitude[None]])
    faults = jnp.pad(faults, ((0, 5), (0, size - faults.shape[1])), constant_values=-1)

    message, row_part = pl.pallas_call(
        functools.partial(pre_kernel, geometry),
        out_shape=[f32(grid_rows, cols * share + 8, size), f32(8, size)],
        in_specs=[SMEM] + [VMEM] * 4,
        out_specs=[VMEM] * 2,
        name="pre",
    )(place, faults, flat, row_codes, col_codes)
    first = exchange(message, "prow")
    own_share = first[:2, : cols * share].reshape(depth, size)
    sums = jnp.sum(first[:, cols * share : cols * share + cols], axis=0)
    panel_part = first[:2, cols * share + cols]

    weights = col_codes[:1].astype(jnp.float32) * 0.25
    message = jnp.concatenate([own_share, row_part[:rows], panel_part, sums[:1], weights])
    second = exchange(everyone(message, grid_cols), "pcol")
    shares = second[:, :depth]
    row_sums = jnp.sum(second[:, depth : depth + rows], axis=0)
    panel_sum = jnp.sum(second[:, depth + rows : depth + rows + 2], axis=0)
    ends = second[:2, depth + rows + 2 :]
    vectors = jnp.concatenate([ends[:, 0], panel_sum, ends[:, 1]])

    by_row = shares.reshape(fold, grid_rows, depth, size).transpose(1, 0, 2, 3)
    corner = jnp.concatenate(
        [shares[0, :share], shares[1, :share], shares[1, cols * share : cols * share + share]]
    )
    message = jnp.concatenate(
        [
            by_row.reshape(grid_rows, fold * depth, size),
            everyone(jnp.concatenate([own_share, corner]), grid_rows),
        ],
        axis=1,
    )
    third = exchange(message, "prow")

    factored, col_check, row_check, col_message, row_message = pl.pallas_call(
        functools.partial(post_kernel, geometry),
        out_shape=[
            f32(rows * size * cols, size),
            f32(cols, size),
            f32(rows, size),
            f32(grid_rows, 8, size),
            f32(grid_cols, 8, size),
        ],
        in_specs=[SMEM] + [VMEM] * 8,
        out_specs=[VMEM] * 5,
        name="post",
    )(place, faults, third, vectors, row_sums, sums, flat, row_codes, col_codes)

    col_found = jnp.sum(exchange(col_message, "prow"), axis=0)[:cols]
    row_found = jnp.sum(exchange(row_message, "pcol"), axis=0)[:rows]
    col_flags = jnp.max(jnp.abs(col_check - col_found), axis=1)
    row_flags = jnp.max(jnp.abs(row_check - row_found), axis=1)
    return (
        factored.reshape(matrix.shape),
        col_check.reshape(cols, 1, size),
        row_check.reshape(rows, 1, size),
        col_flags.reshape(cols, 1),
        row_flags.reshape(rows, 1),
    )


def solution(mesh):
    return jax.shard_map(
        local,
        mesh=mesh,
        in_specs=(
            P(None, "prow", None, None, "pcol", None),
            P(None, "prow", None),
            P(None, "pcol", None),
            P(),
            P(),
            P(),
        ),
        out_specs=(
            P(None, "prow", None, None, "pcol", None),
            P(None, "pcol", None),
            P(None, "prow", None),
            P(None, "pcol"),
            P(None, "prow"),
        ),
        check_vma=False,
    )
```

time: 199 us -> 147 us (0.74)
  other arithmetic: 55.8 us -> 7.74 us
  Pallas kernels: 0 us -> 24.7 us
  matrix products: 20.9 us -> 0 us
  local copies, waits for them, and re-layouts: 23.6 us -> 7.74 us
  blocking collectives: 37.5 us -> 48.2 us
  starting transfers between devices: 29.7 us -> 24.7 us
  waiting for transfers between devices: 29 us -> 32.3 us
    another operation x13 -> x1, other arithmetic: 46.5 us -> 0.58 us  [local(): place = jnp.stack([grid_row, grid_col]).astype(jnp.int32)]
    pallas_call x0 -> x2, Pallas kernels: none -> 24.7 us  [the longest x1 21.8 us: local(): pl.pallas_call(functools.partial(post_kernel, geometry), out_shape=[f32(r...]
    dot_general x26 -> x0, matrix products: 20.4 us -> none  [dot(): return jnp.einsum(spec, a, b, precision=precise)]
    all_to_all x1 -> x2, blocking collectives: 37.5 us -> 48.2 us  [exchange(): return lax.all_to_all(message, axis, 0, 0, tiled=True)]
    unnamed x76 -> x8, local copies, waits for them, and re-layouts: 12.2 us -> 6.12 us
    all_to_all x4 -> x3, starting transfers between devices: 29.7 us -> 24.7 us  [exchange(): return lax.all_to_all(message, axis, 0, 0, tiled=True)]
    reshape x3 -> x0, local copies, waits for them, and re-layouts: 3.55 us -> none  [the longest x1 2.5 us: local(): dot('fr,fc->rc', hit_rows, hit_cols).reshape(rows, size, cols, size)]
    all_to_all x4 -> x3, waiting for transfers between devices: 29 us -> 32.3 us  [exchange(): return lax.all_to_all(message, axis, 0, 0, tiled=True)]
  transfers between devices with their start and end apart: 4 -> 3, of which waited for: 4 -> 3; matrix products, arithmetic and copies ran while one was open for 7% -> 4% of each run, Pallas kernels for 0% -> 0%
where the time goes in v2:
time: 147 us; the launch traced here: 146 us
  blocking collectives  48.2 us (33%)
  waiting for transfers between devices  32.3 us (22%)
  Pallas kernels  24.7 us (17%)
  starting transfers between devices  24.7 us (17%)
  other arithmetic  7.74 us (5%)
  local copies, waits for them, and re-layouts  7.74 us (5%)
    all_to_all x2, blocking collectives, exchange(): return lax.all_to_all(message, axis, 0, 0, tiled=True)  48.2 us
    all_to_all x3, waiting for transfers between devices, exchange(): return lax.all_to_all(message, axis, 0, 0, tiled=True)  32.3 us
    all_to_all x3, starting transfers between devices, exchange(): return lax.all_to_all(message, axis, 0, 0, tiled=True)  24.7 us
    pallas_call x1, Pallas kernels, local(): pl.pallas_call(functools.partial(post_kernel, geometry), out_shape=[f32(r...  21.8 us
    unnamed x8, local copies, waits for them, and re-layouts  6.12 us
  transfers between devices with their start and end apart: 3, of which 3 were waited for; matrix products, arithmetic and copies ran while one was open for 4% of the time, Pallas kernels for 0%

profile of v2, /device:TPU:1, one launch (start us, length us, event | category | flops | bytes accessed | tf_op | source)
XLA Modules:
  0.0 146.1 jit_solution(8961841046046481901)
XLA Ops:
  0.6 0.7 shift-left_bitcast_fusion
  1.3 1.3 copy.32
  2.6 1.3 copy.31
  3.8 0.6 pad_add_fusion.1.place
  4.4 0.7 add_bitcast_fusion
  5.1 0.6 pad.4.faults
  5.7 2.9 %pre.1 = (f32[16,32,128]{2,1,0:T(8,128)}, f32[8,128]{1,0:T(8,128)}) custom-call(s32[2]{0:T(128)} %pad_add_fusion.1.place, s32[8,128]{1,0:T(8,128)} %pad.4.faults, f32[2304,128]{1,0:T(8,128)} %bitcast.39, s32[6,128]{1,0:T(8,128)} %bitcast.45, s32[3,128]{1,0:T(4,128)} %bitcast.47), custom_call_target="tpu_custom_call" | custom-call | tf_op jit(solution)/shard_map/pre/pallas_call | solution.py:294
  8.6 10.2 %all-to-all-start = ((f32[16,32,128]{2,1,0:T(8,128)}), f32[16,32,128]{2,1,0:T(8,128)S(1)}, u32[]{:S(2)}, u32[]{:S(2)}) async-start(f32[16,32,128]{2,1,0:T(8,128)} %get-tuple-element.12), calls=%async_computation | async-start | bytes 524288 | tf_op jit(solution)/shard_map/all_to_all | solution.py:18
  18.8 0.7 multiply_bitcast_fusion
  19.5 6.6 %all-to-all-done = f32[16,32,128]{2,1,0:T(8,128)S(1)} async-done(((f32[16,32,128]{2,1,0:T(8,128)}), f32[16,32,128]{2,1,0:T(8,128)S(1)}, u32[]{:S(2)}, u32[]{:S(2)}) %all-to-all-start) | async-done | bytes 262176 | tf_op jit(solution)/shard_map/all_to_all | solution.py:18
  26.1 0.0 copy-start.1
  26.1 0.7 concatenate.16
  26.9 0.1 broadcast_in_dim.7
  27.0 38.1 %all_to_all.25 = f32[32,58,128]{2,1,0:T(8,128)S(1)} all-to-all(f32[32,58,128]{2,1,0:T(8,128)S(1)} %broadcast_in_dim.7), channel_id=1, replica_groups=mesh['prow'=16,'pcol'=32] {'pcol'}, dimensions={0} | all-to-all | bytes 1900544 | tf_op jit(solution)/shard_map/all_to_all | solution.py:18
  65.1 0.0 copy-done.1
  65.1 0.1 slice.74
  65.1 0.1 copy.19
  65.3 1.2 pad_maximum_fusion
  66.5 7.5 %all-to-all-start.2 = ((f32[16,168,128]{2,1,0:T(8,128)}), f32[16,168,128]{2,1,0:T(8,128)S(1)}, u32[]{:S(2)}, u32[]{:S(2)}) async-start(f32[16,168,128]{2,1,0:T(8,128)} %pad_maximum_fusion), calls=%async_computation.2 | async-start | bytes 2752512 | tf_op jit(solution)/shard_map/all_to_all | solution.py:18
  74.0 0.6 pad_maximum_fusion.2.vectors
  74.6 0.6 slice_reduce_fusion.row_sums
  75.2 18.2 %all-to-all-done.2.third = f32[16,168,128]{2,1,0:T(8,128)S(1)} async-done(((f32[16,168,128]{2,1,0:T(8,128)}), f32[16,168,128]{2,1,0:T(8,128)S(1)}, u32[]{:S(2)}, u32[]{:S(2)}) %all-to-all-start.2) | async-done | bytes 1376288 | tf_op jit(solution)/shard_map/all_to_all | solution.py:18
  93.5 0.0 copy-start
  93.5 1.1 copy-done
  94.5 21.8 %post.1 = (f32[2304,128]{1,0:T(8,128)}, f32[3,128]{1,0:T(4,128)}, f32[6,128]{1,0:T(8,128)}, f32[16,8,128]{2,1,0:T(8,128)}, f32[32,8,128]{2,1,0:T(8,128)}) custom-call(s32[2]{0:T(128)} %pad_add_fusion.1.place, s32[8,128]{1,0:T(8,128)} %pad.4.faults, f32[16,168,128]{2,1,0:T(8,128)} %copy-done, f32[6,128]{1,0:T(8,128)} %pad_maximum_fusion.2.vectors, ...), custom_call_target="tpu_custom_call" | custom-call | tf_op jit(solution)/shard_map/post/pallas_call | solution.py:328
  116.3 10.1 %all_to_all.26 = f32[16,8,128]{2,1,0:T(8,128)S(1)} all-to-all(f32[16,8,128]{2,1,0:T(8,128)} %get-tuple-element.17), channel_id=1, replica_groups=mesh['prow'=16,'pcol'=32] {'prow'}, dimensions={0} | all-to-all | bytes 131072 | tf_op jit(solution)/shard_map/all_to_all | solution.py:18
  126.4 7.0 %all-to-all-start.4 = ((f32[32,8,128]{2,1,0:T(8,128)}), f32[32,8,128]{2,1,0:T(8,128)S(1)}, u32[]{:S(2)}, u32[]{:S(2)}) async-start(f32[32,8,128]{2,1,0:T(8,128)} %get-tuple-element.18), calls=%async_computation.4 | async-start | bytes 262144 | tf_op jit(solution)/shard_map/all_to_all | solution.py:18
  133.5 1.2 copy.23
  134.7 1.3 copy.24
  136.0 1.3 abs_reduce_fusion.1
  137.3 7.5 %all-to-all-done.4 = f32[32,8,128]{2,1,0:T(8,128)S(1)} async-done(((f32[32,8,128]{2,1,0:T(8,128)}), f32[32,8,128]{2,1,0:T(8,128)S(1)}, u32[]{:S(2)}, u32[]{:S(2)}) %all-to-all-start.4) | async-done | bytes 131104 | tf_op jit(solution)/shard_map/all_to_all | solution.py:18
  144.8 1.3 abs_reduce_fusion
  (12 shorter events, 0.2 us)
Async XLA Ops:
  8.6 17.4 %all-to-all-start = ((f32[16,32,128]{2,1,0:T(8,128)}), f32[16,32,128]{2,1,0:T(8,128)S(1)}, u32[]{:S(2)}, u32[]{:S(2)}) async-start(f32[16,32,128]{2,1,0:T(8,128)} %get-tuple-element.12), calls=%async_computation | async-start | bytes 524288 | tf_op jit(solution)/shard_map/all_to_all | solution.py:18
  26.1 39.0 %copy-start.1 = (f32[3,128]{1,0:T(4,128)}, f32[3,128]{1,0:T(4,128)S(1)}, u32[]{:S(2)}) copy-start(f32[3,128]{1,0:T(4,128)S(1)} %slice_reduce_fusion.2.col_sums) | copy-start | bytes 4612
  66.5 27.0 %all-to-all-start.2 = ((f32[16,168,128]{2,1,0:T(8,128)}), f32[16,168,128]{2,1,0:T(8,128)S(1)}, u32[]{:S(2)}, u32[]{:S(2)}) async-start(f32[16,168,128]{2,1,0:T(8,128)} %pad_maximum_fusion), calls=%async_computation.2 | async-start | bytes 2752512 | tf_op jit(solution)/shard_map/all_to_all | solution.py:18
  93.5 1.1 copy-start
  126.4 18.3 %all-to-all-start.4 = ((f32[32,8,128]{2,1,0:T(8,128)}), f32[32,8,128]{2,1,0:T(8,128)S(1)}, u32[]{:S(2)}, u32[]{:S(2)}) async-start(f32[32,8,128]{2,1,0:T(8,128)} %get-tuple-element.18), calls=%async_computation.4 | async-start | bytes 262144 | tf_op jit(solution)/shard_map/all_to_all | solution.py:18

commit v3 on v2

--- a/solution.py
+++ b/solution.py
@@ -98,12 +98,32 @@
     )
 
 
-def pre_kernel(geometry, place, faults, matrix, row_codes, col_codes, message, row_part):
+def stacked_rows(ref):
+    return jnp.concatenate([ref[i] for i in range(ref.shape[0])])
+
+
+def pre_kernel(
+    geometry,
+    place,
+    fault_tiles,
+    fault_cells,
+    fault_bits,
+    matrix,
+    row_codes,
+    col_codes,
+    message,
+    row_part,
+    faults,
+):
     rows, cols, grid_rows, grid_cols = geometry
     grid_row, grid_col = place[0], place[1]
     share = SIZE // grid_rows
-    row_weights = row_codes[...].astype(jnp.float32) * 0.25
-    col_weights = col_codes[...].astype(jnp.float32) * 0.25
+    count = fault_bits.shape[1]
+    faults[...] = jnp.full((8, SIZE), -1, jnp.int32)
+    faults[0:2, 0:count] = fault_tiles[...] * SIZE + fault_cells[...]
+    faults[2:3, 0:count] = jnp.left_shift(jnp.ones((1, count), jnp.int32), fault_bits[...] - 1)
+    row_weights = stacked_rows(row_codes).astype(jnp.float32) * 0.25
+    col_weights = stacked_rows(col_codes).astype(jnp.float32) * 0.25
     turned = columns_of(row_weights)
     ones = jnp.ones((8, SIZE), jnp.float32)
     fault_row, fault_col = faults[0:1, :], faults[1:2, :]
@@ -134,40 +154,20 @@
         message[i, cols * share : cols * share + 8, :] = sums
 
 
-def post_kernel(
-    geometry,
-    place,
-    faults,
-    third,
-    vectors,
-    row_sums,
-    col_sums,
-    matrix,
-    row_codes,
-    col_codes,
-    factored,
-    col_check,
-    row_check,
-    col_message,
-    row_message,
-):
-    rows, cols, grid_rows, grid_cols = geometry
-    grid_row, grid_col = place[0], place[1]
+def factor_kernel(geometry, corners, vectors, transform, uppers, pair):
+    grid_rows = geometry[2]
     share = SIZE // grid_rows
-    fold = grid_cols // grid_rows
-    depth = 2 * cols * share
-
     def gathered(start):
-        return jnp.concatenate([third[i, start : start + share, :] for i in range(grid_rows)])
-
-    corner = [gathered((fold + 1) * depth + k * share) for k in range(3)]
+        return jnp.concatenate([corners[i, start : start + share, :] for i in range(grid_rows)])
+
+    corner = [gathered(k * share) for k in range(3)]
     tile_0 = (corner[0] + corner[0].T) * 0.5
     upper_0, inverse_0 = factor_tile(tile_0)
     below_0 = mm(inverse_0, corner[1])
     tile_1 = corner[2] - mm(below_0.T, below_0)
     upper_1, inverse_1 = factor_tile((tile_1 + tile_1.T) * 0.5)
     mixed = -mm(inverse_1, mm(below_0.T, inverse_0))
-    transform = jnp.concatenate(
+    whole = jnp.concatenate(
         [
             jnp.concatenate([inverse_0, jnp.zeros_like(inverse_0)], axis=1),
             jnp.concatenate([mixed, inverse_1], axis=1),
@@ -186,14 +186,49 @@
             pad,
         ]
     )
-    solved = mm_nt(stacked, transform)
-    new = solved[0:1]
+    solved = mm_nt(stacked, whole)
     shift_0 = solved[1:2, :SIZE] + mm_nt(weight_0, upper_0) - weight_0
     shift_1 = solved[2:3, SIZE:] + mm_nt(weight_1, upper_1) - weight_1
     shift = jnp.concatenate([shift_0, shift_1], axis=1)
-
-    row_weights = row_codes[...].astype(jnp.float32) * 0.25
-    col_weights = col_codes[...].astype(jnp.float32) * 0.25
+    transform[...] = whole
+    uppers[0] = upper_0
+    uppers[1] = upper_1
+    pair[...] = jnp.concatenate([solved[0:1], shift, jnp.zeros((6, 2 * SIZE), jnp.float32)])
+
+
+def post_kernel(
+    geometry,
+    place,
+    faults,
+    third,
+    transform,
+    uppers,
+    pair,
+    row_part,
+    col_sums,
+    matrix,
+    row_codes,
+    col_codes,
+    factored,
+    col_check,
+    row_shift,
+    col_message,
+    row_message,
+):
+    rows, cols, grid_rows, grid_cols = geometry
+    grid_row, grid_col = place[0], place[1]
+    share = SIZE // grid_rows
+    fold = grid_cols // grid_rows
+    depth = 2 * cols * share
+
+    def gathered(start):
+        return jnp.concatenate([third[i, start : start + share, :] for i in range(grid_rows)])
+
+    transform = transform[...]
+    upper_0, upper_1 = uppers[0], uppers[1]
+    new, shift = pair[0:1, :], pair[1:2, :]
+    row_weights = stacked_rows(row_codes).astype(jnp.float32) * 0.25
+    col_weights = stacked_rows(col_codes).astype(jnp.float32) * 0.25
     turned = columns_of(row_weights)
     ones = jnp.ones((8, SIZE), jnp.float32)
     fault_row, fault_col = faults[0:1, :], faults[1:2, :]
@@ -219,7 +254,7 @@
         if u == 0:
             checked = jnp.where(grid_col == 0, new[:, :SIZE], checked)
             checked = jnp.where(grid_col == 1, new[:, SIZE:], checked)
-        col_check[u : u + 1, :] = checked
+        col_check[u] = checked
 
     found = [jnp.zeros((SIZE, SIZE), jnp.float32) for _ in range(cols)]
     found_rows = []
@@ -241,7 +276,7 @@
                     jnp.where(grid_row == 1, upper_1, panel[SIZE:]),
                 ]
             )
-        row_check[t : t + 1, :] = row_sums[t : t + 1, :] - mm(shift, full)
+        row_shift[t] = mm(shift, full)
         upright = panel.T
         row_hits = hits(fault_row, (t * grid_rows + grid_row) * SIZE, magnitude)
         total = jnp.zeros((SIZE, SIZE), jnp.float32)
@@ -267,7 +302,8 @@
     for i in range(grid_rows):
         col_message[i] = found_cols
     for i in range(grid_cols):
-        row_message[i] = found_rows
+        row_message[i, 0:8, :] = found_rows
+        row_message[i, 8:16, :] = row_part[...]
 
 
 def local(matrix, row_codes, col_codes, fault_tiles, fault_cells, fault_bits):
@@ -283,69 +319,75 @@
     f32 = lambda *shape: jax.ShapeDtypeStruct(shape, jnp.float32)
 
     flat = matrix.reshape(rows * size * cols, size)
-    row_codes = row_codes.reshape(rows, size)
-    col_codes = col_codes.reshape(cols, size)
     place = jnp.stack([grid_row, grid_col]).astype(jnp.int32)
-    spots = fault_tiles.T * size + fault_cells.T
-    magnitude = jnp.left_shift(1, fault_bits - 1)
-    faults = jnp.concatenate([spots, magnitude[None]])
-    faults = jnp.pad(faults, ((0, 5), (0, size - faults.shape[1])), constant_values=-1)
-
-    message, row_part = pl.pallas_call(
+
+    message, row_part, faults = pl.pallas_call(
         functools.partial(pre_kernel, geometry),
-        out_shape=[f32(grid_rows, cols * share + 8, size), f32(8, size)],
-        in_specs=[SMEM] + [VMEM] * 4,
-        out_specs=[VMEM] * 2,
+        out_shape=[
+            f32(grid_rows, cols * share + 8, size),
+            f32(8, size),
+            jax.ShapeDtypeStruct((8, size), jnp.int32),
+        ],
+        in_specs=[SMEM] + [VMEM] * 6,
+        out_specs=[VMEM] * 3,
         name="pre",
-    )(place, faults, flat, row_codes, col_codes)
+    )(place, fault_tiles.T, fault_cells.T, fault_bits[None], flat, row_codes, col_codes)
     first = exchange(message, "prow")
     own_share = first[:2, : cols * share].reshape(depth, size)
     sums = jnp.sum(first[:, cols * share : cols * share + cols], axis=0)
     panel_part = first[:2, cols * share + cols]
 
-    weights = col_codes[:1].astype(jnp.float32) * 0.25
-    message = jnp.concatenate([own_share, row_part[:rows], panel_part, sums[:1], weights])
+    weights = col_codes[0].astype(jnp.float32) * 0.25
+    message = jnp.concatenate([own_share, panel_part, sums[:1], weights])
     second = exchange(everyone(message, grid_cols), "pcol")
     shares = second[:, :depth]
-    row_sums = jnp.sum(second[:, depth : depth + rows], axis=0)
-    panel_sum = jnp.sum(second[:, depth + rows : depth + rows + 2], axis=0)
-    ends = second[:2, depth + rows + 2 :]
+    panel_sum = jnp.sum(second[:, depth : depth + 2], axis=0)
+    ends = second[:2, depth + 2 :]
     vectors = jnp.concatenate([ends[:, 0], panel_sum, ends[:, 1]])
 
-    by_row = shares.reshape(fold, grid_rows, depth, size).transpose(1, 0, 2, 3)
     corner = jnp.concatenate(
         [shares[0, :share], shares[1, :share], shares[1, cols * share : cols * share + share]]
     )
+    corners = exchange(everyone(corner, grid_rows), "prow")
+    by_row = shares.reshape(fold, grid_rows, depth, size).transpose(1, 0, 2, 3)
     message = jnp.concatenate(
-        [
-            by_row.reshape(grid_rows, fold * depth, size),
-            everyone(jnp.concatenate([own_share, corner]), grid_rows),
-        ],
-        axis=1,
-    )
+        [by_row.reshape(grid_rows, fold * depth, size), everyone(own_share, grid_rows)], axis=1
+    )
+    message, corners = lax.optimization_barrier((message, corners))
     third = exchange(message, "prow")
-
-    factored, col_check, row_check, col_message, row_message = pl.pallas_call(
+    transform, uppers, pair = pl.pallas_call(
+        functools.partial(factor_kernel, geometry),
+        out_shape=[f32(2 * size, 2 * size), f32(2, size, size), f32(8, 2 * size)],
+        in_specs=[VMEM] * 2,
+        out_specs=[VMEM] * 3,
+        name="factor",
+    )(corners, vectors)
+
+    factored, col_check, row_shift, col_message, row_message = pl.pallas_call(
         functools.partial(post_kernel, geometry),
         out_shape=[
             f32(rows * size * cols, size),
-            f32(cols, size),
-            f32(rows, size),
+            f32(cols, 1, size),
+            f32(rows, 1, size),
             f32(grid_rows, 8, size),
-            f32(grid_cols, 8, size),
+            f32(grid_cols, 16, size),
         ],
-        in_specs=[SMEM] + [VMEM] * 8,
+        in_specs=[SMEM] + [VMEM] * 10,
         out_specs=[VMEM] * 5,
         name="post",
-    )(place, faults, third, vectors, row_sums, sums, flat, row_codes, col_codes)
-
-    col_found = jnp.sum(exchange(col_message, "prow"), axis=0)[:cols]
-    row_found = jnp.sum(exchange(row_message, "pcol"), axis=0)[:rows]
-    col_flags = jnp.max(jnp.abs(col_check - col_found), axis=1)
-    row_flags = jnp.max(jnp.abs(row_check - row_found), axis=1)
+    )(place, faults, third, transform, uppers, pair, row_part, sums, flat, row_codes, col_codes)
+
+    row_found = exchange(row_message, "pcol")
+    col_message, row_found = lax.optimization_barrier((col_message, row_found))
+    col_found = exchange(col_message, "prow")
+    row_found = jnp.sum(row_found, axis=0)
+    row_check = row_found[8 : 8 + rows] - row_shift.reshape(rows, size)
+    row_flags = jnp.max(jnp.abs(row_check - row_found[:rows]), axis=1)
+    col_found = jnp.sum(col_found, axis=0)[:cols]
+    col_flags = jnp.max(jnp.abs(col_check.reshape(cols, size) - col_found), axis=1)
     return (
         factored.reshape(matrix.shape),
-        col_check.reshape(cols, 1, size),
+        col_check,
         row_check.reshape(rows, 1, size),
         col_flags.reshape(cols, 1),
         row_flags.reshape(rows, 1),

time: 147 us -> 139 us (0.946)
  waiting for transfers between devices: 32.3 us -> 20.3 us
  blocking collectives: 48.2 us -> 55.7 us
  local copies, waits for them, and re-layouts: 7.74 us -> 2.51 us
  starting transfers between devices: 24.7 us -> 27.4 us
  other arithmetic: 7.74 us -> 5.71 us
  Pallas kernels: 24.7 us -> 26.2 us
    pallas_call x0 -> x1, Pallas kernels: none -> 12.3 us  [local(): pl.pallas_call(functools.partial(factor_kernel, geometry), out_shape=[f32...]
    all_to_all x3 -> x4, waiting for transfers between devices: 32.3 us -> 20.3 us  [exchange(): return lax.all_to_all(message, axis, 0, 0, tiled=True)]
    pallas_call x1, Pallas kernels: 21.8 us -> 11 us  [local(): pl.pallas_call(functools.partial(post_kernel, geometry), out_shape=[f32(r...]
    all_to_all x2, blocking collectives: 48.2 us -> 55.7 us  [exchange(): return lax.all_to_all(message, axis, 0, 0, tiled=True)]
    unnamed x8 -> x7, local copies, waits for them, and re-layouts: 6.12 us -> 1.6 us
    all_to_all x3 -> x4, starting transfers between devices: 24.7 us -> 27.4 us  [exchange(): return lax.all_to_all(message, axis, 0, 0, tiled=True)]
  transfers between devices with their start and end apart: 3 -> 4, of which waited for: 3 -> 4; matrix products, arithmetic and copies ran while one was open for 4% -> 3% of each run, Pallas kernels for 0% -> 9%
where the time goes in v3:
time: 139 us
  blocking collectives  55.7 us (40%)
  starting transfers between devices  27.4 us (20%)
  Pallas kernels  26.2 us (19%)
  waiting for transfers between devices  20.3 us (15%)
  other arithmetic  5.71 us (4%)
  local copies, waits for them, and re-layouts  2.51 us (2%)
    all_to_all x2, blocking collectives, exchange(): return lax.all_to_all(message, axis, 0, 0, tiled=True)  55.7 us
    all_to_all x4, starting transfers between devices, exchange(): return lax.all_to_all(message, axis, 0, 0, tiled=True)  27.4 us
    all_to_all x4, waiting for transfers between devices, exchange(): return lax.all_to_all(message, axis, 0, 0, tiled=True)  20.3 us
    pallas_call x1, Pallas kernels, local(): pl.pallas_call(functools.partial(factor_kernel, geometry), out_shape=[f32...  12.3 us
    pallas_call x1, Pallas kernels, local(): pl.pallas_call(functools.partial(post_kernel, geometry), out_shape=[f32(r...  11 us
    pallas_call x1, Pallas kernels, local(): pl.pallas_call(functools.partial(pre_kernel, geometry), out_shape=[f32(gr...  2.93 us
  transfers between devices with their start and end apart: 4, of which 4 were waited for; matrix products, arithmetic and copies ran while one was open for 3% of the time, Pallas kernels for 9%

profile of v3, /device:TPU:1, one launch (start us, length us, event | category | flops | bytes accessed | tf_op | source)
XLA Modules:
  0.0 138.6 jit_solution(17448015203842237929)
XLA Ops:
  0.6 0.6 pad_add_fusion.place
  1.2 2.9 %pre.1 = (f32[16,32,128]{2,1,0:T(8,128)}, f32[8,128]{1,0:T(8,128)}, s32[8,128]{1,0:T(8,128)}) custom-call(s32[2]{0:T(128)} %pad_add_fusion.place, s32[2,96]{1,0:T(2,128)} %bitcast.52, s32[2,96]{1,0:T(2,128)} %bitcast.53, s32[1,96]{1,0:T(1,128)} %bitcast.54, f32[2304,128]{1,0:T(8,128)} %bitcast.43, s32[6,1,128]{2,1,0:T(1,128)} %row_codes.3, ...), custom_call_target="tpu_custom_call" | custom-call | tf_op jit(solution)/shard_map/pre/pallas_call | solution.py:324
  4.2 10.2 %all-to-all-start = ((f32[16,32,128]{2,1,0:T(8,128)}), f32[16,32,128]{2,1,0:T(8,128)S(1)}, u32[]{:S(2)}, u32[]{:S(2)}) async-start(f32[16,32,128]{2,1,0:T(8,128)} %get-tuple-element.21), calls=%async_computation | async-start | bytes 524288 | tf_op jit(solution)/shard_map/all_to_all | solution.py:18
  14.4 0.7 multiply_bitcast_fusion
  15.0 6.6 %all-to-all-done = f32[16,32,128]{2,1,0:T(8,128)S(1)} async-done(((f32[16,32,128]{2,1,0:T(8,128)}), f32[16,32,128]{2,1,0:T(8,128)S(1)}, u32[]{:S(2)}, u32[]{:S(2)}) %all-to-all-start) | async-done | bytes 262176 | tf_op jit(solution)/shard_map/all_to_all | solution.py:18
  21.6 0.0 copy-start.2
  21.7 0.1 broadcast_in_dim.9
  21.8 36.3 %all_to_all.30 = f32[32,52,128]{2,1,0:T(8,128)S(1)} all-to-all(f32[32,52,128]{2,1,0:T(8,128)S(1)} %broadcast_in_dim.9), channel_id=1, replica_groups=mesh['prow'=16,'pcol'=32] {'pcol'}, dimensions={0} | all-to-all | bytes 1703936 | tf_op jit(solution)/shard_map/all_to_all | solution.py:18
  58.1 0.0 copy-done.2
  58.1 0.7 broadcast_in_dim.11
  58.8 6.5 %all-to-all-start.2 = ((f32[16,24,128]{2,1,0:T(8,128)}), f32[16,24,128]{2,1,0:T(8,128)S(1)}, u32[]{:S(2)}, u32[]{:S(2)}) async-start(f32[16,24,128]{2,1,0:T(8,128)} %broadcast_in_dim.11), calls=%async_computation.2 | async-start | bytes 393216 | tf_op jit(solution)/shard_map/all_to_all | solution.py:18
  65.3 0.1 slice.69
  65.3 0.1 copy.21
  65.4 1.1 pad_maximum_fusion
  66.5 5.4 %all-to-all-done.2.corners = f32[16,24,128]{2,1,0:T(8,128)S(1)} async-done(((f32[16,24,128]{2,1,0:T(8,128)}), f32[16,24,128]{2,1,0:T(8,128)S(1)}, u32[]{:S(2)}, u32[]{:S(2)}) %all-to-all-start.2) | async-done | bytes 196640 | tf_op jit(solution)/shard_map/all_to_all | solution.py:18
  72.0 0.0 copy-start.1
  72.0 4.3 %all-to-all-start.3 = ((f32[16,144,128]{2,1,0:T(8,128)}), f32[16,144,128]{2,1,0:T(8,128)S(1)}, u32[]{:S(2)}, u32[]{:S(2)}) async-start(f32[16,144,128]{2,1,0:T(8,128)} %pad_maximum_fusion), calls=%async_computation.3 | async-start | bytes 2359296 | tf_op jit(solution)/shard_map/all_to_all | solution.py:18
  76.3 0.0 copy-done.1
  76.3 0.6 pad_maximum_fusion.3.vectors
  76.9 12.3 %factor.1 = (f32[256,256]{1,0:T(8,128)}, f32[2,128,128]{2,1,0:T(8,128)}, f32[8,256]{1,0:T(8,128)}) custom-call(f32[16,24,128]{2,1,0:T(8,128)} %copy-done.1, f32[6,128]{1,0:T(8,128)} %pad_maximum_fusion.3.vectors), custom_call_target="tpu_custom_call" | custom-call | tf_op jit(solution)/shard_map/factor/pallas_call | solution.py:358
  89.2 4.4 %all-to-all-done.3.third = f32[16,144,128]{2,1,0:T(8,128)S(1)} async-done(((f32[16,144,128]{2,1,0:T(8,128)}), f32[16,144,128]{2,1,0:T(8,128)S(1)}, u32[]{:S(2)}, u32[]{:S(2)}) %all-to-all-start.3) | async-done | bytes 1179680 | tf_op jit(solution)/shard_map/all_to_all | solution.py:18
  93.6 0.0 copy-start
  93.6 1.0 copy-done
  94.6 11.0 %post.1 = (f32[2304,128]{1,0:T(8,128)}, f32[3,1,128]{2,1,0:T(1,128)}, f32[6,1,128]{2,1,0:T(1,128)}, f32[16,8,128]{2,1,0:T(8,128)}, f32[32,16,128]{2,1,0:T(8,128)}) custom-call(s32[2]{0:T(128)} %pad_add_fusion.place, s32[8,128]{1,0:T(8,128)} %get-tuple-element.20.faults, f32[16,144,128]{2,1,0:T(8,128)} %copy-done, f32[256,256]{1,0:T(8,128)} %get-tuple-element.24.transform, ...), custom_call_target="tpu_custom_call" | custom-call | tf_op jit(solution)/shard_map/post/pallas_call | solution.py:366
  105.6 19.4 %all_to_all.31 = f32[32,16,128]{2,1,0:T(8,128)S(1)} all-to-all(f32[32,16,128]{2,1,0:T(8,128)} %get-tuple-element.31), channel_id=1, replica_groups=mesh['prow'=16,'pcol'=32] {'pcol'}, dimensions={0} | all-to-all | bytes 524288 | tf_op jit(solution)/shard_map/all_to_all | solution.py:18
  125.0 6.5 %all-to-all-start.5 = ((f32[16,8,128]{2,1,0:T(8,128)}), f32[16,8,128]{2,1,0:T(8,128)S(1)}, u32[]{:S(2)}, u32[]{:S(2)}) async-start(f32[16,8,128]{2,1,0:T(8,128)} %get-tuple-element.34), calls=%async_computation.5 | async-start | bytes 131072 | tf_op jit(solution)/shard_map/all_to_all | solution.py:18
  131.5 1.3 fusion.1
  132.8 0.6 copy.25
  133.4 3.9 %all-to-all-done.5 = f32[16,8,128]{2,1,0:T(8,128)S(1)} async-done(((f32[16,8,128]{2,1,0:T(8,128)}), f32[16,8,128]{2,1,0:T(8,128)S(1)}, u32[]{:S(2)}, u32[]{:S(2)}) %all-to-all-start.5) | async-done | bytes 65568 | tf_op jit(solution)/shard_map/all_to_all | solution.py:18
  137.3 1.3 fusion.3
  (12 shorter events, 0.2 us)
Async XLA Ops:
  4.2 17.4 %all-to-all-start = ((f32[16,32,128]{2,1,0:T(8,128)}), f32[16,32,128]{2,1,0:T(8,128)S(1)}, u32[]{:S(2)}, u32[]{:S(2)}) async-start(f32[16,32,128]{2,1,0:T(8,128)} %get-tuple-element.21), calls=%async_computation | async-start | bytes 524288 | tf_op jit(solution)/shard_map/all_to_all | solution.py:18
  21.6 36.5 %copy-start.2 = (f32[3,128]{1,0:T(4,128)}, f32[3,128]{1,0:T(4,128)S(1)}, u32[]{:S(2)}) copy-start(f32[3,128]{1,0:T(4,128)S(1)} %slice_reduce_fusion.1.col_sums) | copy-start | bytes 4612
  58.8 13.1 %all-to-all-start.2 = ((f32[16,24,128]{2,1,0:T(8,128)}), f32[16,24,128]{2,1,0:T(8,128)S(1)}, u32[]{:S(2)}, u32[]{:S(2)}) async-start(f32[16,24,128]{2,1,0:T(8,128)} %broadcast_in_dim.11), calls=%async_computation.2 | async-start | bytes 393216 | tf_op jit(solution)/shard_map/all_to_all | solution.py:18
  72.0 4.3 %copy-start.1 = (f32[16,24,128]{2,1,0:T(8,128)}, f32[16,24,128]{2,1,0:T(8,128)S(1)}, u32[]{:S(2)}) copy-start(f32[16,24,128]{2,1,0:T(8,128)S(1)} %all-to-all-done.2.corners) | copy-start | bytes 589828
  72.0 21.6 %all-to-all-start.3 = ((f32[16,144,128]{2,1,0:T(8,128)}), f32[16,144,128]{2,1,0:T(8,128)S(1)}, u32[]{:S(2)}, u32[]{:S(2)}) async-start(f32[16,144,128]{2,1,0:T(8,128)} %pad_maximum_fusion), calls=%async_computation.3 | async-start | bytes 2359296 | tf_op jit(solution)/shard_map/all_to_all | solution.py:18
  93.6 1.0 copy-start
  125.0 12.3 %all-to-all-start.5 = ((f32[16,8,128]{2,1,0:T(8,128)}), f32[16,8,128]{2,1,0:T(8,128)S(1)}, u32[]{:S(2)}, u32[]{:S(2)}) async-start(f32[16,8,128]{2,1,0:T(8,128)} %get-tuple-element.34), calls=%async_computation.5 | async-start | bytes 131072 | tf_op jit(solution)/shard_map/all_to_all | solution.py:18

commit v4 on v3

--- a/solution.py
+++ b/solution.py
@@ -198,6 +198,7 @@
 
 def post_kernel(
     geometry,
+    early,
     place,
     faults,
     third,
@@ -294,7 +295,9 @@
             total = total + tile * col_weights[u : u + 1]
             found[u] = found[u] + tile * turned[t]
         found_rows.append(mm_nt(ones, total)[0:1])
-    found_rows.append(jnp.zeros((8 - rows, SIZE), jnp.float32))
+    found_rows.append(row_part[early:rows, :])
+    if (2 * rows - early) % 8:
+        found_rows.append(jnp.zeros(((early - 2 * rows) % 8, SIZE), jnp.float32))
     found_rows = jnp.concatenate(found_rows)
     found_cols = [jnp.sum(found[u], axis=0, keepdims=True) for u in range(cols)]
     found_cols.append(jnp.zeros((8 - cols, SIZE), jnp.float32))
@@ -302,8 +305,7 @@
     for i in range(grid_rows):
         col_message[i] = found_cols
     for i in range(grid_cols):
-        row_message[i, 0:8, :] = found_rows
-        row_message[i, 8:16, :] = row_part[...]
+        row_message[i] = found_rows
 
 
 def local(matrix, row_codes, col_codes, fault_tiles, fault_cells, fault_bits):
@@ -338,11 +340,13 @@
     panel_part = first[:2, cols * share + cols]
 
     weights = col_codes[0].astype(jnp.float32) * 0.25
-    message = jnp.concatenate([own_share, panel_part, sums[:1], weights])
+    early = min(rows - 1, -(depth + 4) % 8)
+    message = jnp.concatenate([own_share, panel_part, sums[:1], weights, row_part[:early]])
     second = exchange(everyone(message, grid_cols), "pcol")
     shares = second[:, :depth]
     panel_sum = jnp.sum(second[:, depth : depth + 2], axis=0)
-    ends = second[:2, depth + 2 :]
+    ends = second[:2, depth + 2 : depth + 4]
+    early_sums = jnp.sum(second[:, depth + 4 :], axis=0)
     vectors = jnp.concatenate([ends[:, 0], panel_sum, ends[:, 1]])
 
     corner = jnp.concatenate(
@@ -364,13 +368,13 @@
     )(corners, vectors)
 
     factored, col_check, row_shift, col_message, row_message = pl.pallas_call(
-        functools.partial(post_kernel, geometry),
+        functools.partial(post_kernel, geometry, early),
         out_shape=[
             f32(rows * size * cols, size),
             f32(cols, 1, size),
             f32(rows, 1, size),
             f32(grid_rows, 8, size),
-            f32(grid_cols, 16, size),
+            f32(grid_cols, 2 * rows - early + (early - 2 * rows) % 8, size),
         ],
         in_specs=[SMEM] + [VMEM] * 10,
         out_specs=[VMEM] * 5,
@@ -381,7 +385,8 @@
     col_message, row_found = lax.optimization_barrier((col_message, row_found))
     col_found = exchange(col_message, "prow")
     row_found = jnp.sum(row_found, axis=0)
-    row_check = row_found[8 : 8 + rows] - row_shift.reshape(rows, size)
+    row_sums = jnp.concatenate([early_sums, row_found[rows : 2 * rows - early]])
+    row_check = row_sums - row_shift.reshape(rows, size)
     row_flags = jnp.max(jnp.abs(row_check - row_found[:rows]), axis=1)
     col_found = jnp.sum(col_found, axis=0)[:cols]
     col_flags = jnp.max(jnp.abs(col_check.reshape(cols, size) - col_found), axis=1)

time: 139 us -> 138 us (level)
  blocking collectives: 55.7 us -> 36.3 us
  waiting for transfers between devices: 20.3 us -> 30.4 us
  starting transfers between devices: 27.4 us -> 33.8 us
    all_to_all x2 -> x1, blocking collectives: 55.7 us -> 36.3 us  [exchange(): return lax.all_to_all(message, axis, 0, 0, tiled=True)]
    all_to_all x4 -> x5, waiting for transfers between devices: 20.3 us -> 30.4 us  [exchange(): return lax.all_to_all(message, axis, 0, 0, tiled=True)]
    all_to_all x4 -> x5, starting transfers between devices: 27.4 us -> 33.8 us  [exchange(): return lax.all_to_all(message, axis, 0, 0, tiled=True)]
  transfers between devices with their start and end apart: 4 -> 5, of which waited for: 4 -> 5; matrix products, arithmetic and copies ran while one was open for 3% -> 4% of each run, Pallas kernels for 9% -> 9%
where the time goes in v4:
time: 138 us; the launch traced here: 137 us
  blocking collectives  36.3 us (26%)
  starting transfers between devices  33.8 us (24%)
  waiting for transfers between devices  30.4 us (22%)
  Pallas kernels  26.2 us (19%)
  other arithmetic  6.42 us (5%)
  local copies, waits for them, and re-layouts  3.21 us (2%)
    all_to_all x1, blocking collectives, exchange(): return lax.all_to_all(message, axis, 0, 0, tiled=True)  36.3 us
    all_to_all x5, starting transfers between devices, exchange(): return lax.all_to_all(message, axis, 0, 0, tiled=True)  33.8 us
    all_to_all x5, waiting for transfers between devices, exchange(): return lax.all_to_all(message, axis, 0, 0, tiled=True)  30.4 us
    pallas_call x1, Pallas kernels, local(): pl.pallas_call(functools.partial(factor_kernel, geometry), out_shape=[f32...  12.3 us
    pallas_call x1, Pallas kernels, local(): pl.pallas_call(functools.partial(post_kernel, geometry, early), out_shape...  11 us
    pallas_call x1, Pallas kernels, local(): pl.pallas_call(functools.partial(pre_kernel, geometry), out_shape=[f32(gr...  2.93 us
  transfers between devices with their start and end apart: 5, of which 5 were waited for; matrix products, arithmetic and copies ran while one was open for 4% of the time, Pallas kernels for 9%

profile of v4, /device:TPU:1, one launch (start us, length us, event | category | flops | bytes accessed | tf_op | source)
XLA Modules:
  0.0 137.1 jit_solution(6674172101109194707)
XLA Ops:
  0.6 0.6 pad_add_fusion.place
  1.2 2.9 %pre.1 = (f32[16,32,128]{2,1,0:T(8,128)}, f32[8,128]{1,0:T(8,128)}, s32[8,128]{1,0:T(8,128)}) custom-call(s32[2]{0:T(128)} %pad_add_fusion.place, s32[2,96]{1,0:T(2,128)} %bitcast.58, s32[2,96]{1,0:T(2,128)} %bitcast.59, s32[1,96]{1,0:T(1,128)} %bitcast.60, f32[2304,128]{1,0:T(8,128)} %bitcast.48, s32[6,1,128]{2,1,0:T(1,128)} %row_codes.3, ...), custom_call_target="tpu_custom_call" | custom-call | tf_op jit(solution)/shard_map/pre/pallas_call | solution.py:326
  4.2 10.2 %all-to-all-start = ((f32[16,32,128]{2,1,0:T(8,128)}), f32[16,32,128]{2,1,0:T(8,128)S(1)}, u32[]{:S(2)}, u32[]{:S(2)}) async-start(f32[16,32,128]{2,1,0:T(8,128)} %get-tuple-element.21), calls=%async_computation | async-start | bytes 524288 | tf_op jit(solution)/shard_map/all_to_all | solution.py:18
  14.4 0.7 slice.62
  15.0 0.7 multiply_bitcast_fusion
  15.7 5.9 %all-to-all-done = f32[16,32,128]{2,1,0:T(8,128)S(1)} async-done(((f32[16,32,128]{2,1,0:T(8,128)}), f32[16,32,128]{2,1,0:T(8,128)S(1)}, u32[]{:S(2)}, u32[]{:S(2)}) %all-to-all-start) | async-done | bytes 262176 | tf_op jit(solution)/shard_map/all_to_all | solution.py:18
  21.6 0.0 copy-start.2
  21.7 0.1 broadcast_in_dim.9
  21.8 36.3 %all_to_all.30 = f32[32,56,128]{2,1,0:T(8,128)S(1)} all-to-all(f32[32,56,128]{2,1,0:T(8,128)S(1)} %broadcast_in_dim.9), channel_id=1, replica_groups=mesh['prow'=16,'pcol'=32] {'pcol'}, dimensions={0} | all-to-all | bytes 1835008 | tf_op jit(solution)/shard_map/all_to_all | solution.py:18
  58.1 0.0 copy-done.2
  58.1 0.7 broadcast_in_dim.11
  58.8 6.5 %all-to-all-start.2 = ((f32[16,24,128]{2,1,0:T(8,128)}), f32[16,24,128]{2,1,0:T(8,128)S(1)}, u32[]{:S(2)}, u32[]{:S(2)}) async-start(f32[16,24,128]{2,1,0:T(8,128)} %broadcast_in_dim.11), calls=%async_computation.2 | async-start | bytes 393216 | tf_op jit(solution)/shard_map/all_to_all | solution.py:18
  65.3 0.1 slice.77
  65.3 0.1 copy.23
  65.4 1.1 pad_maximum_fusion
  66.5 5.4 %all-to-all-done.2.corners = f32[16,24,128]{2,1,0:T(8,128)S(1)} async-done(((f32[16,24,128]{2,1,0:T(8,128)}), f32[16,24,128]{2,1,0:T(8,128)S(1)}, u32[]{:S(2)}, u32[]{:S(2)}) %all-to-all-start.2) | async-done | bytes 196640 | tf_op jit(solution)/shard_map/all_to_all | solution.py:18
  72.0 0.0 copy-start.1
  72.0 4.3 %all-to-all-start.3 = ((f32[16,144,128]{2,1,0:T(8,128)}), f32[16,144,128]{2,1,0:T(8,128)S(1)}, u32[]{:S(2)}, u32[]{:S(2)}) async-start(f32[16,144,128]{2,1,0:T(8,128)} %pad_maximum_fusion), calls=%async_computation.3 | async-start | bytes 2359296 | tf_op jit(solution)/shard_map/all_to_all | solution.py:18
  76.3 0.0 copy-done.1
  76.3 0.6 pad_maximum_fusion.2.vectors
  76.9 12.3 %factor.1 = (f32[256,256]{1,0:T(8,128)}, f32[2,128,128]{2,1,0:T(8,128)}, f32[8,256]{1,0:T(8,128)}) custom-call(f32[16,24,128]{2,1,0:T(8,128)} %copy-done.1, f32[6,128]{1,0:T(8,128)} %pad_maximum_fusion.2.vectors), custom_call_target="tpu_custom_call" | custom-call | tf_op jit(solution)/shard_map/factor/pallas_call | solution.py:362
  89.1 4.4 %all-to-all-done.3.third = f32[16,144,128]{2,1,0:T(8,128)S(1)} async-done(((f32[16,144,128]{2,1,0:T(8,128)}), f32[16,144,128]{2,1,0:T(8,128)S(1)}, u32[]{:S(2)}, u32[]{:S(2)}) %all-to-all-start.3) | async-done | bytes 1179680 | tf_op jit(solution)/shard_map/all_to_all | solution.py:18
  93.6 0.0 copy-start
  93.6 1.0 copy-done
  94.6 11.0 %post.1 = (f32[2304,128]{1,0:T(8,128)}, f32[3,1,128]{2,1,0:T(1,128)}, f32[6,1,128]{2,1,0:T(1,128)}, f32[16,8,128]{2,1,0:T(8,128)}, f32[32,8,128]{2,1,0:T(8,128)}) custom-call(s32[2]{0:T(128)} %pad_add_fusion.place, s32[8,128]{1,0:T(8,128)} %get-tuple-element.20.faults, f32[16,144,128]{2,1,0:T(8,128)} %copy-done, f32[256,256]{1,0:T(8,128)} %get-tuple-element.25.transform, ...), custom_call_target="tpu_custom_call" | custom-call | tf_op jit(solution)/shard_map/post/pallas_call | solution.py:370
  105.6 7.5 %all-to-all-start.4 = ((f32[32,8,128]{2,1,0:T(8,128)}), f32[32,8,128]{2,1,0:T(8,128)S(1)}, u32[]{:S(2)}, u32[]{:S(2)}) async-start(f32[32,8,128]{2,1,0:T(8,128)} %get-tuple-element.31), calls=%async_computation.4 | async-start | bytes 262144 | tf_op jit(solution)/shard_map/all_to_all | solution.py:18
  113.1 11.3 %all-to-all-done.4 = f32[32,8,128]{2,1,0:T(8,128)S(1)} async-done(((f32[32,8,128]{2,1,0:T(8,128)}), f32[32,8,128]{2,1,0:T(8,128)S(1)}, u32[]{:S(2)}, u32[]{:S(2)}) %all-to-all-start.4) | async-done | bytes 131104 | tf_op jit(solution)/shard_map/all_to_all | solution.py:18
  124.5 5.4 %all-to-all-start.5 = ((f32[16,8,128]{2,1,0:T(8,128)}), f32[16,8,128]{2,1,0:T(8,128)S(1)}, u32[]{:S(2)}, u32[]{:S(2)}) async-start(f32[16,8,128]{2,1,0:T(8,128)} %get-tuple-element.34), calls=%async_computation.5 | async-start | bytes 131072 | tf_op jit(solution)/shard_map/all_to_all | solution.py:18
  129.9 0.7 copy_subtract_fusion
  130.6 0.6 copy.28
  131.2 1.3 fusion.3
  132.5 3.3 %all-to-all-done.5 = f32[16,8,128]{2,1,0:T(8,128)S(1)} async-done(((f32[16,8,128]{2,1,0:T(8,128)}), f32[16,8,128]{2,1,0:T(8,128)S(1)}, u32[]{:S(2)}, u32[]{:S(2)}) %all-to-all-start.5) | async-done | bytes 65568 | tf_op jit(solution)/shard_map/all_to_all | solution.py:18
  135.8 1.3 fusion.5
  (14 shorter events, 0.2 us)
Async XLA Ops:
  4.2 17.4 %all-to-all-start = ((f32[16,32,128]{2,1,0:T(8,128)}), f32[16,32,128]{2,1,0:T(8,128)S(1)}, u32[]{:S(2)}, u32[]{:S(2)}) async-start(f32[16,32,128]{2,1,0:T(8,128)} %get-tuple-element.21), calls=%async_computation | async-start | bytes 524288 | tf_op jit(solution)/shard_map/all_to_all | solution.py:18
  21.6 36.5 %copy-start.2 = (f32[3,128]{1,0:T(4,128)}, f32[3,128]{1,0:T(4,128)S(1)}, u32[]{:S(2)}) copy-start(f32[3,128]{1,0:T(4,128)S(1)} %slice_reduce_fusion.2.col_sums) | copy-start | bytes 4612
  58.8 13.1 %all-to-all-start.2 = ((f32[16,24,128]{2,1,0:T(8,128)}), f32[16,24,128]{2,1,0:T(8,128)S(1)}, u32[]{:S(2)}, u32[]{:S(2)}) async-start(f32[16,24,128]{2,1,0:T(8,128)} %broadcast_in_dim.11), calls=%async_computation.2 | async-start | bytes 393216 | tf_op jit(solution)/shard_map/all_to_all | solution.py:18
  72.0 4.3 %copy-start.1 = (f32[16,24,128]{2,1,0:T(8,128)}, f32[16,24,128]{2,1,0:T(8,128)S(1)}, u32[]{:S(2)}) copy-start(f32[16,24,128]{2,1,0:T(8,128)S(1)} %all-to-all-done.2.corners) | copy-start | bytes 589828
  72.0 21.6 %all-to-all-start.3 = ((f32[16,144,128]{2,1,0:T(8,128)}), f32[16,144,128]{2,1,0:T(8,128)S(1)}, u32[]{:S(2)}, u32[]{:S(2)}) async-start(f32[16,144,128]{2,1,0:T(8,128)} %pad_maximum_fusion), calls=%async_computation.3 | async-start | bytes 2359296 | tf_op jit(solution)/shard_map/all_to_all | solution.py:18
  93.6 1.0 copy-start
  105.6 18.9 %all-to-all-start.4 = ((f32[32,8,128]{2,1,0:T(8,128)}), f32[32,8,128]{2,1,0:T(8,128)S(1)}, u32[]{:S(2)}, u32[]{:S(2)}) async-start(f32[32,8,128]{2,1,0:T(8,128)} %get-tuple-element.31), calls=%async_computation.4 | async-start | bytes 262144 | tf_op jit(solution)/shard_map/all_to_all | solution.py:18
  124.5 11.3 %all-to-all-start.5 = ((f32[16,8,128]{2,1,0:T(8,128)}), f32[16,8,128]{2,1,0:T(8,128)S(1)}, u32[]{:S(2)}, u32[]{:S(2)}) async-start(f32[16,8,128]{2,1,0:T(8,128)} %get-tuple-element.34), calls=%async_computation.5 | async-start | bytes 131072 | tf_op jit(solution)/shard_map/all_to_all | solution.py:18
